TPU v7x, 256 devices: a whole 4x4x8 slice. The times are simulated.
256 devices in a mesh: sec: 4 (over z_lo), row: 8 (over x, core), col: 8 (over y, z_hi).
Axes of the slice: x: 4, y: 4, z: 8 (z_hi: 2, z_lo: 4; z = z_hi * 4 + z_lo), core: 2. Of those that a mesh axis runs over, the one named last changes fastest.
Arguments:
- amps: bfloat16 [16, 32, 32, 512], P(None, ('sec', 'row'), 'col'), may hold values from -6 to 6
- driver: bfloat16 [16, 32, 32, 512], P(None, 'col', ('sec', 'row')), may hold values from -6 to 6
- ladder_operator: bfloat16 [16384, 16384], P('col', ('sec', 'row')), as said below
- ladder_block_mask: int32 [128, 128], P('col', ('sec', 'row')), may hold values from 0 to 1, as said below
- cycle_op: bfloat16 [16384, 16384], P(('sec', 'row'), 'col'), as said below
- cycle_mask: int32 [128, 128], P(('sec', 'row'), 'col'), may hold values from 0 to 1, as said below
- occ_i: float32 [16], replicated, may hold values from -2 to -0.3
- occ_j: float32 [32], replicated, may hold values from -2 to -0.3
- vir_a: float32 [32], replicated, may hold values from 0.2 to 3
- vir_b: float32 [512], replicated, may hold values from 0.2 to 3
Outputs:
- amp_one: float32 [16, 32, 32, 512], P(None, 'col', ('sec', 'row'))
- amp_two: float32 [16, 32, 32, 512], P(None, ('sec', 'row'), 'col')
Inputs may be any that keep to these rules, and one draw needn't show every extreme that they name: ladder_operator is symmetric. cycle_op is symmetric. ladder_block_mask is symmetric with ones on its diagonal. cycle_mask is symmetric with ones on its diagonal.
All inputs are finite; a program needn't handle non-finite values.
Results may differ from a plain program's by a relative error of at most 0.0024.
Values may be sent and summed in bfloat16 or wider, within the bound.
No kernel may reach another device: no remote copies, remote signals or barrier semaphores. Data moves between devices by JAX's collectives and lax.ppermute only.
A program may use at most 64 MiB of HBM per device.

v0:
```python
import jax
import jax.numpy as jnp
from jax import lax
from jax.experimental import pallas as pl
from jax.experimental.pallas import tpu as pltpu
from jax.sharding import Mesh
from jax.sharding import PartitionSpec as P


AXES = ("sec", "rx", "core", "y", "zh")
WIDE = ("sec", "rx", "core")
COLS = ("y", "zh")
F32 = jnp.float32
BF16 = jnp.bfloat16
SHIFTS = (1, 3, 2)
FLIPS = (1, 2, 3)


def shifted(x, axis, step):
    n = lax.axis_size(axis)
    return lax.ppermute(x, axis, [(i, (i + step) % n) for i in range(n)])


def flipped(x, axis, mask):
    n = lax.axis_size(axis)
    return lax.ppermute(x, axis, [(i, i ^ mask) for i in range(n)])


def swapped(x, axes):
    n = 2 ** len(axes)
    return lax.ppermute(x, axes, [(i, n - 1 - i) for i in range(n)])


def vmem(n):
    return [pl.BlockSpec(memory_space=pltpu.VMEM)] * n


def smem(n):
    return [pl.BlockSpec(memory_space=pltpu.SMEM)] * n


LIMIT = pltpu.CompilerParams(vmem_limit_bytes=16 * 2**20)


def on_chip(*arrays):
    return [pltpu.with_memory_space_constraint(x, pltpu.VMEM) for x in arrays]


def sds(shape, dtype):
    return pltpu.VMEM(shape, dtype)


def mask_tile(tile, mask, turned):
    rows, cols = mask.shape
    edge_r = tile.shape[0] // rows
    edge_c = tile.shape[1] // cols

    def kernel(mask_ref, tile_ref, out_ref):
        p = pl.program_id(0)
        start = pl.multiple_of(p * edge_r, edge_r)
        for q in range(cols):
            cut = pl.ds(q * edge_c, edge_c)
            value = mask_ref[q, p] if turned else mask_ref[p, q]
            out_ref[pl.ds(start, edge_r), cut] = tile_ref[:, cut] * value.astype(F32).astype(BF16)

    return pl.pallas_call(
        kernel,
        grid=(rows,),
        out_shape=sds(tile.shape, tile.dtype),
        in_specs=smem(1) + [pl.BlockSpec((edge_r, tile.shape[1]), lambda p: (p, 0))],
        out_specs=vmem(1)[0],
        compiler_params=LIMIT,
        name="mask_tile",
    )(mask.T if turned else mask, tile)


def joined(parts):
    def kernel(*refs):
        out = refs[-1]
        for n, ref in enumerate(refs[:-1]):
            out[n] = ref[...]

    return pl.pallas_call(
        kernel,
        out_shape=sds((len(parts), *parts[0].shape), parts[0].dtype),
        in_specs=vmem(len(parts)),
        out_specs=vmem(1)[0],
        compiler_params=LIMIT,
        name="joined",
    )(*on_chip(*parts))


def dot(rows, tile, transposed):
    dims = (((1,), (1 if transposed else 0,)), ((), ()))
    return lax.dot_general(rows, tile, dims, preferred_element_type=F32)


def place():
    return [lax.axis_index(name) for name in AXES]


def wide_product(parts, tiles, transposed, wire):
    _, r_count, i_count, d_count = parts[0].shape
    n_cols = tiles[0].shape[0] if transposed else tiles[0].shape[1]

    def kernel(*refs):
        ins = refs[:4]
        tile_refs = refs[4:6]
        outs = refs[6:10]
        rows_ref = refs[10]
        z, x, _, y, zh = place()
        for s in range(4):
            xs = (x + 4 - s) % 4
            for m in range(4):
                zs = z ^ m
                at = (((zs + 4 - y) % 4) * 2 + ((xs // 2) ^ zh)) * 2 + xs % 2
                for r in range(r_count):
                    rows_ref[r, at] = ins[s][m, r]
        for q in range(2):
            acc = None
            for r in range(r_count):
                rows = rows_ref[r].reshape(16 * i_count, d_count)
                cut = pl.ds(r * d_count, d_count)
                part = dot(rows, tile_refs[q][:, cut] if transposed else tile_refs[q][cut, :], transposed)
                acc = part if acc is None else acc + part
            acc = acc.reshape(4, 2, 2, i_count, n_cols)
            for s in range(4):
                outs[s][:, q] = acc[s].astype(outs[s].dtype)

    shape = (2, 2, 2, i_count, n_cols)
    return pl.pallas_call(
        kernel,
        out_shape=[sds(shape, F32 if s == 0 else wire) for s in range(4)],
        in_specs=vmem(6),
        out_specs=vmem(4),
        scratch_shapes=[pltpu.VMEM((r_count, 16, i_count, d_count), BF16)],
        compiler_params=LIMIT,
        name="wide_product",
    )(*on_chip(*parts, *tiles))


def cols_product(parts, tiles, transposed, wire):
    i_count, d_count = parts[0].shape[-2:]
    cuts = (tiles[0].shape[0] if transposed else tiles[0].shape[1]) // d_count

    def kernel(*refs):
        ins = refs[:4]
        tile_refs = refs[4:6]
        outs = refs[6:10]
        rows_ref = refs[10]
        z, x, _, y, zh = place()
        for s in range(4):
            ys = (y + 4 - s) % 4
            for q in range(2):
                for half in range(2):
                    xs = (zh ^ q) * 2 + half
                    at = ((xs + 4 - x) % 4) * 4 + (ys ^ z)
                    for k in range(2):
                        rows_ref[k, at] = ins[s][q, k, half]

        @pl.loop(0, cuts)
        def _(n):
            cut = pl.ds(pl.multiple_of(n * d_count, d_count), d_count)
            acc = None
            for k in range(2):
                rows = rows_ref[k].reshape(16 * i_count, d_count)
                part = dot(rows, tile_refs[k][cut, :] if transposed else tile_refs[k][:, cut], transposed)
                acc = part if acc is None else acc + part
            acc = acc.reshape(4, 4, i_count, d_count)
            for s in range(4):
                outs[s][:, n] = acc[s].astype(outs[s].dtype)

    shape = (4, cuts, i_count, d_count)
    return pl.pallas_call(
        kernel,
        out_shape=[sds(shape, F32 if s == 0 else wire) for s in range(4)],
        in_specs=vmem(6),
        out_specs=vmem(4),
        scratch_shapes=[pltpu.VMEM((2, 16, i_count, d_count), BF16)],
        compiler_params=LIMIT,
        name="cols_product",
    )(*on_chip(*parts, *tiles))


def summed(arrays, wire, depth):
    lead = arrays[0].shape[:depth]
    inside = arrays[0].shape[depth:]
    places = [()]
    for size in lead:
        places = [at + (n,) for at in places for n in range(size)]

    def kernel(*refs):
        ins = refs[: len(arrays)]
        outs = refs[len(arrays) :]
        for out, at in zip(outs, places):
            total = ins[0][at].astype(F32)
            for ref in ins[1:]:
                total = total + ref[at].astype(F32)
            out[...] = total.astype(out.dtype)

    return pl.pallas_call(
        kernel,
        out_shape=[sds(inside, F32 if n == 0 else wire) for n in range(len(places))],
        in_specs=vmem(len(arrays)),
        out_specs=vmem(len(places)),
        compiler_params=LIMIT,
        name="summed",
    )(*on_chip(*arrays))


def finished(base, whole, near, far, energies, swap, onward):
    n_base, n_whole, n_near = len(base), len(whole), len(near)
    r_count, i_count, d_count = whole[0].shape

    def kernel(*refs):
        refs = list(refs)

        def take(n):
            taken = refs[:n]
            del refs[:n]
            return taken

        occ_i, occ_j, vir_a, vir_b = take(4)
        bases, wholes, halves = take(n_base), take(n_whole), (take(n_near), take(n_near))
        outs, (stage,) = take(len(shapes)), take(1)
        z, x, core, y, zh = place()
        wide, cols = (z * 4 + x) * 2 + core, y * 2 + zh
        row = lax.broadcasted_iota(jnp.int32, (i_count, d_count), 0)
        occ = jnp.zeros((i_count, d_count), F32)
        for i in range(i_count):
            occ = jnp.where(row == i, occ_i[i], occ)
        for ref in bases:
            for r in range(r_count):
                stage[r] = ref[:, r, :].astype(F32)
        for k in range(2):
            for half in range(2):
                r = half * 2 + (core ^ k)
                total = wholes[0][r].astype(F32)
                for ref in wholes[1:]:
                    total = total + ref[r].astype(F32)
                for ref in halves[k]:
                    total = total + ref[half].astype(F32)
                if n_base:
                    total = total + stage[r]
                place_j, place_a = (cols * r_count + r, wide) if swap else (wide, cols * r_count + r)
                total = total / (vir_a[place_a] + vir_b[...] - occ - occ_j[place_j])
                stage[r] = total
                if onward:
                    rounded = total.astype(BF16)
                    outs[1][r] = rounded
                    outs[2 + k][half] = rounded
        for r in range(r_count):
            outs[0][:, r, :] = stage[r]

    shapes = [jax.ShapeDtypeStruct((i_count, r_count, d_count), F32)]
    if onward:
        shapes += [sds((r_count, i_count, d_count), BF16)] + [sds((r_count // 2, i_count, d_count), BF16)] * 2
    return pl.pallas_call(
        kernel,
        out_shape=shapes,
        in_specs=smem(3) + vmem(n_base + n_whole + 2 * n_near + 1),
        out_specs=vmem(len(shapes)),
        scratch_shapes=[pltpu.VMEM((r_count, i_count, d_count), F32)],
        compiler_params=LIMIT,
        name="finished",
    )(*energies[:3], *on_chip(energies[3][None], *base, *whole, *near, *far))


def prepared(amps):
    i_count, r_count, d_count = amps.shape

    def kernel(in_ref, all_ref, near_ref, far_ref):
        core = lax.axis_index("core")
        for r in range(r_count):
            all_ref[r] = in_ref[:, r, :]
        for half in range(r_count // 2):
            near_ref[half] = all_ref[half * 2 + core]
            far_ref[half] = all_ref[half * 2 + (core ^ 1)]

    return pl.pallas_call(
        kernel,
        out_shape=[sds((r_count, i_count, d_count), BF16)] + [sds((r_count // 2, i_count, d_count), BF16)] * 2,
        in_specs=vmem(1),
        out_specs=vmem(3),
        compiler_params=LIMIT,
        name="prepared",
    )(*on_chip(amps))


def wide_gather(piece):
    parts = joined([piece] + [flipped(piece, "sec", m) for m in FLIPS])
    here = {0: parts}
    for s in SHIFTS:
        here[s] = shifted(parts, "rx", s)
    return [here[s] for s in range(4)]


def cols_gather(near, far):
    zh = swapped(near, ("zh",))
    both = swapped(far, ("core", "zh"))
    core = swapped(far, ("core",))
    parts = joined([near, core, zh, both])
    parts = parts.reshape(2, 2, *parts.shape[1:])
    here = {0: parts}
    for s in SHIFTS:
        here[s] = shifted(parts, "y", s)
    return [here[s] for s in range(4)]


def cols_sum(outs, wire):
    arrays = [outs[0]] + [shifted(outs[s], "y", s) for s in SHIFTS]
    own, core, zh, both = summed(arrays, wire, 2)
    near = [own, swapped(zh, ("zh",))]
    far = [swapped(core, ("core",)), swapped(both, ("core", "zh"))]
    return near, far


def wide_sum(outs, wire):
    arrays = [outs[0]] + [shifted(outs[s], "rx", s) for s in SHIFTS]
    parts = summed(arrays, wire, 1)
    return [parts[0]] + [flipped(parts[m], "sec", m) for m in FLIPS]


def sweep(piece, near, far, wide_tiles, cols_tiles, transposed, wire):
    wide_parts = wide_gather(piece)
    cols_parts = cols_gather(near, far)
    outs = cols_product(cols_parts, cols_tiles, transposed, wire)
    whole = wide_sum(outs, wire)
    outs = wide_product(wide_parts, wide_tiles, transposed, wire)
    near, far = cols_sum(outs, wire)
    return whole, near, far


def body(
    amps,
    driver,
    ladder_operator,
    ladder_block_mask,
    cycle_op,
    cycle_mask,
    occ_i,
    occ_j,
    vir_a,
    vir_b,
):
    energies = (occ_i, occ_j, vir_a, vir_b)
    start = prepared(amps[:, 0])
    cycle_tile = mask_tile(cycle_op, cycle_mask, False)
    ladder_tile = mask_tile(ladder_operator, ladder_block_mask, True)
    cycle_tiles = (cycle_tile, swapped(cycle_tile, ("core",)))
    ladder_tiles = (ladder_tile, swapped(ladder_tile, ("core",)))
    sums = sweep(*start, ladder_tiles, cycle_tiles, False, F32)
    amp_one, *start = finished([driver[:, :, 0]], *sums, energies, True, True)
    sums = sweep(*start, cycle_tiles, ladder_tiles, True, BF16)
    (amp_two,) = finished([], *sums, energies, False, False)
    return amp_one[:, :, None], amp_two[:, None]


def solution(mesh):
    split = Mesh(mesh.devices.reshape(4, 4, 2, 4, 2), AXES)
    return jax.shard_map(
        body,
        mesh=split,
        in_specs=(
            P(None, WIDE, COLS, None),
            P(None, COLS, WIDE, None),
            P(COLS, WIDE),
            P(COLS, WIDE),
            P(WIDE, COLS),
            P(WIDE, COLS),
            P(),
            P(),
            P(),
            P(),
        ),
        out_specs=(P(None, COLS, WIDE, None), P(None, WIDE, COLS, None)),
        check_vma=False,
    )
```

profile of v0, /device:TPU:8, one launch (start us, length us, event | category | flops | bytes accessed | tf_op | source)
XLA Modules:
  0.0 152.1 jit_solution(2401823326045722257)
XLA Ops:
  0.6 1.6 %copy-done = bf16[2048,512]{1,0:T(8,128)(2,1)S(1)} copy-done((bf16[2048,512]{1,0:T(8,128)(2,1)S(1)}, bf16[2048,512]{1,0:T(8,128)(2,1)}, u32[]{:S(2)}) %copy-start) | copy-done | bytes 2097176
  2.9 1.4 mask_tile.3.refs_4_
  6.3 4.7 %collective-permute-start.15 = (bf16[4,16,512]{2,1,0:T(8,128)(2,1)S(1)}, bf16[4,16,512]{2,1,0:T(8,128)(2,1)S(1)}, u32[]{:S(2)}, u32[]{:S(2)}) collective-permute-start(bf16[4,16,512]{2,1,0:T(8,128)(2,1)S(1)} %get-tuple-element.51.refs_0_), channel_id=1, source_target_pairs={{0,192},{64,128},{128,64},{192,0},{1,193},{65,129},{129,65},{193,1... | collective-permute-start | bytes 196616 | tf_op jit(solution)/shard_map/ppermute | solution.py:26
  11.7 2.1 %collective-permute-done.15.refs_3_ = bf16[4,16,512]{2,1,0:T(8,128)(2,1)S(1)} collective-permute-done((bf16[4,16,512]{2,1,0:T(8,128)(2,1)S(1)}, bf16[4,16,512]{2,1,0:T(8,128)(2,1)S(1)}, u32[]{:S(2)}, u32[]{:S(2)}) %collective-permute-start.15) | collective-permute-done | bytes 65568 | tf_op jit(solution)/shard_map/ppermute | solution.py:26
  13.8 6.6 %collective-permute-start.1 = (bf16[2,16,512]{2,1,0:T(8,128)(2,1)S(1)}, bf16[2,16,512]{2,1,0:T(8,128)(2,1)S(1)}, u32[]{:S(2)}, u32[]{:S(2)}) collective-permute-start(bf16[2,16,512]{2,1,0:T(8,128)(2,1)S(1)} %get-tuple-element.41.refs_0_), channel_id=1, source_target_pairs={{0,1},{1,0},{2,3},{3,2},{4,5},{5,4},{6,7},{7,6},{8,9},{9,8},{10,11... | collective-permute-start | bytes 98312 | tf_op jit(solution)/shard_map/ppermute | solution.py:31
  20.4 1.7 %collective-permute-start.2 = (bf16[2,16,512]{2,1,0:T(8,128)(2,1)S(1)}, bf16[2,16,512]{2,1,0:T(8,128)(2,1)S(1)}, u32[]{:S(2)}, u32[]{:S(2)}) collective-permute-start(bf16[2,16,512]{2,1,0:T(8,128)(2,1)S(1)} %get-tuple-element.42), channel_id=1, source_target_pairs={{0,9},{1,8},{8,1},{9,0},{2,11},{3,10},{10,3},{11,2},{4,13},{5,12},... | collective-permute-start | bytes 98312 | tf_op jit(solution)/shard_map/ppermute | solution.py:31
  22.7 2.8 %collective-permute-start.18 = (bf16[4,4,16,512]{3,2,1,0:T(8,128)(2,1)S(1)}, bf16[4,4,16,512]{3,2,1,0:T(8,128)(2,1)S(1)}, u32[]{:S(2)}, u32[]{:S(2)}) collective-permute-start(bf16[4,4,16,512]{3,2,1,0:T(8,128)(2,1)S(1)} %joined.5.refs_0_), channel_id=1, source_target_pairs={{0,48},{16,0},{32,16},{48,32},{1,49},{17,1},{33,17},{49,33},{2,50}... | collective-permute-start | bytes 786440 | tf_op jit(solution)/shard_map/ppermute | solution.py:21
  25.5 2.1 %collective-permute-done.2.refs_3_ = bf16[2,16,512]{2,1,0:T(8,128)(2,1)S(1)} collective-permute-done((bf16[2,16,512]{2,1,0:T(8,128)(2,1)S(1)}, bf16[2,16,512]{2,1,0:T(8,128)(2,1)S(1)}, u32[]{:S(2)}, u32[]{:S(2)}) %collective-permute-start.2) | collective-permute-done | bytes 32800 | tf_op jit(solution)/shard_map/ppermute | solution.py:31
  27.7 3.0 %collective-permute-start.17 = (bf16[4,4,16,512]{3,2,1,0:T(8,128)(2,1)S(1)}, bf16[4,4,16,512]{3,2,1,0:T(8,128)(2,1)S(1)}, u32[]{:S(2)}, u32[]{:S(2)}) collective-permute-start(bf16[4,4,16,512]{3,2,1,0:T(8,128)(2,1)S(1)} %joined.5.refs_0_), channel_id=1, source_target_pairs={{0,32},{16,48},{32,0},{48,16},{1,33},{17,49},{33,1},{49,17},{2,34}... | collective-permute-start | bytes 786440 | tf_op jit(solution)/shard_map/ppermute | solution.py:21
  31.3 5.6 %collective-permute-done.18.refs_3_ = bf16[4,4,16,512]{3,2,1,0:T(8,128)(2,1)S(1)} collective-permute-done((bf16[4,4,16,512]{3,2,1,0:T(8,128)(2,1)S(1)}, bf16[4,4,16,512]{3,2,1,0:T(8,128)(2,1)S(1)}, u32[]{:S(2)}, u32[]{:S(2)}) %collective-permute-start.18) | collective-permute-done | bytes 262176 | tf_op jit(solution)/shard_map/ppermute | solution.py:21
  38.3 2.3 %collective-permute-start.4 = (bf16[2,2,2,16,512]{4,3,2,1,0:T(8,128)(2,1)S(1)}, bf16[2,2,2,16,512]{4,3,2,1,0:T(8,128)(2,1)S(1)}, u32[]{:S(2)}, u32[]{:S(2)}) collective-permute-start(bf16[2,2,2,16,512]{4,3,2,1,0:T(8,128)(2,1)S(1)} %bitcast.11), channel_id=1, source_target_pairs={{0,4},{2,6},{4,0},{6,2},{1,5},{3,7},{5,1},{7,3},{8,12},{10,14},{12... | collective-permute-start | bytes 393224 | tf_op jit(solution)/shard_map/ppermute | solution.py:21
  41.1 1.6 %collective-permute-start.3 = (bf16[2,2,2,16,512]{4,3,2,1,0:T(8,128)(2,1)S(1)}, bf16[2,2,2,16,512]{4,3,2,1,0:T(8,128)(2,1)S(1)}, u32[]{:S(2)}, u32[]{:S(2)}) collective-permute-start(bf16[2,2,2,16,512]{4,3,2,1,0:T(8,128)(2,1)S(1)} %bitcast.12), channel_id=1, source_target_pairs={{0,2},{2,4},{4,6},{6,0},{1,3},{3,5},{5,7},{7,1},{8,10},{10,12},{12... | collective-permute-start | bytes 393224 | tf_op jit(solution)/shard_map/ppermute | solution.py:21
  44.0 1.4 collective-permute-start.20
  45.3 2.8 %collective-permute-done.3.refs_1_ = bf16[2,2,2,16,512]{4,3,2,1,0:T(8,128)(2,1)S(1)} collective-permute-done((bf16[2,2,2,16,512]{4,3,2,1,0:T(8,128)(2,1)S(1)}, bf16[2,2,2,16,512]{4,3,2,1,0:T(8,128)(2,1)S(1)}, u32[]{:S(2)}, u32[]{:S(2)}) %collective-permute-start.3) | collective-permute-done | bytes 131104 | tf_op jit(solution)/shard_map/ppermute | solution.py:21
  48.1 1.8 %cols_product.2 = (f32[4,4,16,512]{3,2,1,0:T(8,128)S(1)}, f32[4,4,16,512]{3,2,1,0:T(8,128)S(1)}, f32[4,4,16,512]{3,2,1,0:T(8,128)S(1)}, f32[4,4,16,512]{3,2,1,0:T(8,128)S(1)}) custom-call(bf16[2,2,2,16,512]{4,3,2,1,0:T(8,128)(2,1)S(1)} %bitcast.13, bf16[2,2,2,16,512]{4,3,2,1,0:T(8,128)(2,1)S(1)} %collective-permute-done.3.refs_1_, ...), custom_call_target="tpu_custom_call" | custom-call | tf_op jit(solution)/shard_map/cols_product/pallas_call | solution.py:174
  50.0 1.7 %collective-permute-start.7 = (f32[4,4,16,512]{3,2,1,0:T(8,128)S(1)}, f32[4,4,16,512]{3,2,1,0:T(8,128)S(1)}, u32[]{:S(2)}, u32[]{:S(2)}) collective-permute-start(f32[4,4,16,512]{3,2,1,0:T(8,128)S(1)} %get-tuple-element.44), channel_id=1, source_target_pairs={{0,16},{16,32},{32,48},{48,0},{1,17},{17,33},{33,49},{49,1},{2,18}... | collective-permute-start | bytes 1572872 | tf_op jit(solution)/shard_map/ppermute | solution.py:21
  51.8 2.1 %collective-permute-start.8 = (f32[4,4,16,512]{3,2,1,0:T(8,128)S(1)}, f32[4,4,16,512]{3,2,1,0:T(8,128)S(1)}, u32[]{:S(2)}, u32[]{:S(2)}) collective-permute-start(f32[4,4,16,512]{3,2,1,0:T(8,128)S(1)} %get-tuple-element.45), channel_id=1, source_target_pairs={{0,48},{16,0},{32,16},{48,32},{1,49},{17,1},{33,17},{49,33},{2,50}... | collective-permute-start | bytes 1572872 | tf_op jit(solution)/shard_map/ppermute | solution.py:21
  55.1 1.8 %collective-permute-start.21 = (f32[2,2,2,16,512]{4,3,2,1,0:T(8,128)S(1)}, f32[2,2,2,16,512]{4,3,2,1,0:T(8,128)S(1)}, u32[]{:S(2)}, u32[]{:S(2)}) collective-permute-start(f32[2,2,2,16,512]{4,3,2,1,0:T(8,128)S(1)} %get-tuple-element.54), channel_id=1, source_target_pairs={{0,6},{2,0},{4,2},{6,4},{1,7},{3,1},{5,3},{7,5},{8,14},{10,8},{12,... | collective-permute-start | bytes 786440 | tf_op jit(solution)/shard_map/ppermute | solution.py:21
  57.6 6.4 %collective-permute-done.21.refs_2_ = f32[2,2,2,16,512]{4,3,2,1,0:T(8,128)S(1)} collective-permute-done((f32[2,2,2,16,512]{4,3,2,1,0:T(8,128)S(1)}, f32[2,2,2,16,512]{4,3,2,1,0:T(8,128)S(1)}, u32[]{:S(2)}, u32[]{:S(2)}) %collective-permute-start.21) | collective-permute-done | bytes 262176 | tf_op jit(solution)/shard_map/ppermute | solution.py:21
  64.0 2.8 %collective-permute-done.22.refs_3_ = f32[2,2,2,16,512]{4,3,2,1,0:T(8,128)S(1)} collective-permute-done((f32[2,2,2,16,512]{4,3,2,1,0:T(8,128)S(1)}, f32[2,2,2,16,512]{4,3,2,1,0:T(8,128)S(1)}, u32[]{:S(2)}, u32[]{:S(2)}) %collective-permute-start.22) | collective-permute-done | bytes 262176 | tf_op jit(solution)/shard_map/ppermute | solution.py:21
  66.9 3.8 %collective-permute-start.23 = (f32[2,16,512]{2,1,0:T(8,128)S(1)}, f32[2,16,512]{2,1,0:T(8,128)S(1)}, u32[]{:S(2)}, u32[]{:S(2)}) collective-permute-start(f32[2,16,512]{2,1,0:T(8,128)S(1)} %get-tuple-element.57), channel_id=1, source_target_pairs={{0,1},{1,0},{2,3},{3,2},{4,5},{5,4},{6,7},{7,6},{8,9},{9,8},{10,11... | collective-permute-start | bytes 196616 | tf_op jit(solution)/shard_map/ppermute | solution.py:31
  70.7 1.9 %collective-permute-done.8.refs_2_ = f32[4,4,16,512]{3,2,1,0:T(8,128)S(1)} collective-permute-done((f32[4,4,16,512]{3,2,1,0:T(8,128)S(1)}, f32[4,4,16,512]{3,2,1,0:T(8,128)S(1)}, u32[]{:S(2)}, u32[]{:S(2)}) %collective-permute-start.8) | collective-permute-done | bytes 524320 | tf_op jit(solution)/shard_map/ppermute | solution.py:21
  72.6 1.6 %collective-permute-done.9.refs_3_ = f32[4,4,16,512]{3,2,1,0:T(8,128)S(1)} collective-permute-done((f32[4,4,16,512]{3,2,1,0:T(8,128)S(1)}, f32[4,4,16,512]{3,2,1,0:T(8,128)S(1)}, u32[]{:S(2)}, u32[]{:S(2)}) %collective-permute-start.9) | collective-permute-done | bytes 524320 | tf_op jit(solution)/shard_map/ppermute | solution.py:21
  75.1 3.7 %collective-permute-start.12 = (f32[4,16,512]{2,1,0:T(8,128)S(1)}, f32[4,16,512]{2,1,0:T(8,128)S(1)}, u32[]{:S(2)}, u32[]{:S(2)}) collective-permute-start(f32[4,16,512]{2,1,0:T(8,128)S(1)} %get-tuple-element.50), channel_id=1, source_target_pairs={{0,192},{64,128},{128,64},{192,0},{1,193},{65,129},{129,65},{193,1... | collective-permute-start | bytes 393224 | tf_op jit(solution)/shard_map/ppermute | solution.py:26
  78.8 5.1 %collective-permute-start.25 = (f32[2,16,512]{2,1,0:T(8,128)S(1)}, f32[2,16,512]{2,1,0:T(8,128)S(1)}, u32[]{:S(2)}, u32[]{:S(2)}) collective-permute-start(f32[2,16,512]{2,1,0:T(8,128)S(1)} %get-tuple-element.59), channel_id=1, source_target_pairs={{0,9},{1,8},{8,1},{9,0},{2,11},{3,10},{10,3},{11,2},{4,13},{5,12},... | collective-permute-start | bytes 196616 | tf_op jit(solution)/shard_map/ppermute | solution.py:31
  83.9 3.3 %collective-permute-done.25.refs_12_ = f32[2,16,512]{2,1,0:T(8,128)S(1)} collective-permute-done((f32[2,16,512]{2,1,0:T(8,128)S(1)}, f32[2,16,512]{2,1,0:T(8,128)S(1)}, u32[]{:S(2)}, u32[]{:S(2)}) %collective-permute-start.25) | collective-permute-done | bytes 65568 | tf_op jit(solution)/shard_map/ppermute | solution.py:31
  89.2 3.3 %collective-permute-start.38 = (bf16[4,16,512]{2,1,0:T(8,128)(2,1)S(1)}, bf16[4,16,512]{2,1,0:T(8,128)(2,1)S(1)}, u32[]{:S(2)}, u32[]{:S(2)}) collective-permute-start(bf16[4,16,512]{2,1,0:T(8,128)(2,1)S(1)} %get-tuple-element.71.refs_0_), channel_id=1, source_target_pairs={{0,64},{64,0},{128,192},{192,128},{1,65},{65,1},{129,193},{193,129... | collective-permute-start | bytes 196616 | tf_op jit(solution)/shard_map/ppermute | solution.py:26
  92.4 4.2 %collective-permute-start.27 = (bf16[2,16,512]{2,1,0:T(8,128)(2,1)S(1)}, bf16[2,16,512]{2,1,0:T(8,128)(2,1)S(1)}, u32[]{:S(2)}, u32[]{:S(2)}) collective-permute-start(bf16[2,16,512]{2,1,0:T(8,128)(2,1)S(1)} %get-tuple-element.61.refs_0_), channel_id=1, source_target_pairs={{0,1},{1,0},{2,3},{3,2},{4,5},{5,4},{6,7},{7,6},{8,9},{9,8},{10,11... | collective-permute-start | bytes 98312 | tf_op jit(solution)/shard_map/ppermute | solution.py:31
  96.6 2.5 %collective-permute-start.28 = (bf16[2,16,512]{2,1,0:T(8,128)(2,1)S(1)}, bf16[2,16,512]{2,1,0:T(8,128)(2,1)S(1)}, u32[]{:S(2)}, u32[]{:S(2)}) collective-permute-start(bf16[2,16,512]{2,1,0:T(8,128)(2,1)S(1)} %get-tuple-element.62), channel_id=1, source_target_pairs={{0,9},{1,8},{8,1},{9,0},{2,11},{3,10},{10,3},{11,2},{4,13},{5,12},... | collective-permute-start | bytes 98312 | tf_op jit(solution)/shard_map/ppermute | solution.py:31
  99.1 2.8 %collective-permute-start.43 = (bf16[4,4,16,512]{3,2,1,0:T(8,128)(2,1)S(1)}, bf16[4,4,16,512]{3,2,1,0:T(8,128)(2,1)S(1)}, u32[]{:S(2)}, u32[]{:S(2)}) collective-permute-start(bf16[4,4,16,512]{3,2,1,0:T(8,128)(2,1)S(1)} %joined.7.refs_0_), channel_id=1, source_target_pairs={{0,48},{16,0},{32,16},{48,32},{1,49},{17,1},{33,17},{49,33},{2,50}... | collective-permute-start | bytes 786440 | tf_op jit(solution)/shard_map/ppermute | solution.py:21
  101.9 2.1 %collective-permute-done.28.refs_3_ = bf16[2,16,512]{2,1,0:T(8,128)(2,1)S(1)} collective-permute-done((bf16[2,16,512]{2,1,0:T(8,128)(2,1)S(1)}, bf16[2,16,512]{2,1,0:T(8,128)(2,1)S(1)}, u32[]{:S(2)}, u32[]{:S(2)}) %collective-permute-start.28) | collective-permute-done | bytes 32800 | tf_op jit(solution)/shard_map/ppermute | solution.py:31
  104.0 5.6 %collective-permute-start.31 = (bf16[2,2,2,16,512]{4,3,2,1,0:T(8,128)(2,1)S(1)}, bf16[2,2,2,16,512]{4,3,2,1,0:T(8,128)(2,1)S(1)}, u32[]{:S(2)}, u32[]{:S(2)}) collective-permute-start(bf16[2,2,2,16,512]{4,3,2,1,0:T(8,128)(2,1)S(1)} %bitcast.14), channel_id=1, source_target_pairs={{0,6},{2,0},{4,2},{6,4},{1,7},{3,1},{5,3},{7,5},{8,14},{10,8},{12,... | collective-permute-start | bytes 393224 | tf_op jit(solution)/shard_map/ppermute | solution.py:21
  109.6 1.6 %collective-permute-start.29 = (bf16[2,2,2,16,512]{4,3,2,1,0:T(8,128)(2,1)S(1)}, bf16[2,2,2,16,512]{4,3,2,1,0:T(8,128)(2,1)S(1)}, u32[]{:S(2)}, u32[]{:S(2)}) collective-permute-start(bf16[2,2,2,16,512]{4,3,2,1,0:T(8,128)(2,1)S(1)} %bitcast.16), channel_id=1, source_target_pairs={{0,2},{2,4},{4,6},{6,0},{1,3},{3,5},{5,7},{7,1},{8,10},{10,12},{12... | collective-permute-start | bytes 393224 | tf_op jit(solution)/shard_map/ppermute | solution.py:21
  112.1 2.0 %collective-permute-start.41 = (bf16[4,4,16,512]{3,2,1,0:T(8,128)(2,1)S(1)}, bf16[4,4,16,512]{3,2,1,0:T(8,128)(2,1)S(1)}, u32[]{:S(2)}, u32[]{:S(2)}) collective-permute-start(bf16[4,4,16,512]{3,2,1,0:T(8,128)(2,1)S(1)} %joined.7.refs_0_), channel_id=1, source_target_pairs={{0,16},{16,32},{32,48},{48,0},{1,17},{17,33},{33,49},{49,1},{2,18}... | collective-permute-start | bytes 786440 | tf_op jit(solution)/shard_map/ppermute | solution.py:21
  114.2 1.8 %collective-permute-done.30.refs_2_ = bf16[2,2,2,16,512]{4,3,2,1,0:T(8,128)(2,1)S(1)} collective-permute-done((bf16[2,2,2,16,512]{4,3,2,1,0:T(8,128)(2,1)S(1)}, bf16[2,2,2,16,512]{4,3,2,1,0:T(8,128)(2,1)S(1)}, u32[]{:S(2)}, u32[]{:S(2)}) %collective-permute-start.30) | collective-permute-done | bytes 131104 | tf_op jit(solution)/shard_map/ppermute | solution.py:21
  116.0 1.9 %cols_product.3 = (f32[4,4,16,512]{3,2,1,0:T(8,128)S(1)}, bf16[4,4,16,512]{3,2,1,0:T(8,128)(2,1)S(1)}, bf16[4,4,16,512]{3,2,1,0:T(8,128)(2,1)S(1)}, bf16[4,4,16,512]{3,2,1,0:T(8,128)(2,1)S(1)}) custom-call(bf16[2,2,2,16,512]{4,3,2,1,0:T(8,128)(2,1)S(1)} %bitcast.17, bf16[2,2,2,16,512]{4,3,2,1,0:T(8,128)(2,1)S(1)} %collective-permute-done.29.refs_1_, ...), custom_call_target="tpu_custom_call" | custom-call | tf_op jit(solution)/shard_map/cols_product/pallas_call | solution.py:174
  118.1 3.2 %collective-permute-start.33 = (bf16[4,4,16,512]{3,2,1,0:T(8,128)(2,1)S(1)}, bf16[4,4,16,512]{3,2,1,0:T(8,128)(2,1)S(1)}, u32[]{:S(2)}, u32[]{:S(2)}) collective-permute-start(bf16[4,4,16,512]{3,2,1,0:T(8,128)(2,1)S(1)} %get-tuple-element.65), channel_id=1, source_target_pairs={{0,48},{16,0},{32,16},{48,32},{1,49},{17,1},{33,17},{49,33},{2,50}... | collective-permute-start | bytes 786440 | tf_op jit(solution)/shard_map/ppermute | solution.py:21
  121.8 3.8 %collective-permute-done.41.refs_1_ = bf16[4,4,16,512]{3,2,1,0:T(8,128)(2,1)S(1)} collective-permute-done((bf16[4,4,16,512]{3,2,1,0:T(8,128)(2,1)S(1)}, bf16[4,4,16,512]{3,2,1,0:T(8,128)(2,1)S(1)}, u32[]{:S(2)}, u32[]{:S(2)}) %collective-permute-start.41) | collective-permute-done | bytes 262176 | tf_op jit(solution)/shard_map/ppermute | solution.py:21
  125.6 1.3 wide_product.3
  127.0 3.2 %collective-permute-start.44 = (bf16[2,2,2,16,512]{4,3,2,1,0:T(8,128)(2,1)S(1)}, bf16[2,2,2,16,512]{4,3,2,1,0:T(8,128)(2,1)S(1)}, u32[]{:S(2)}, u32[]{:S(2)}) collective-permute-start(bf16[2,2,2,16,512]{4,3,2,1,0:T(8,128)(2,1)S(1)} %get-tuple-element.73), channel_id=1, source_target_pairs={{0,2},{2,4},{4,6},{6,0},{1,3},{3,5},{5,7},{7,1},{8,10},{10,12},{12... | collective-permute-start | bytes 393224 | tf_op jit(solution)/shard_map/ppermute | solution.py:21
  130.1 1.3 collective-permute-done.32.refs_1_
  131.4 2.0 %collective-permute-start.46 = (bf16[2,2,2,16,512]{4,3,2,1,0:T(8,128)(2,1)S(1)}, bf16[2,2,2,16,512]{4,3,2,1,0:T(8,128)(2,1)S(1)}, u32[]{:S(2)}, u32[]{:S(2)}) collective-permute-start(bf16[2,2,2,16,512]{4,3,2,1,0:T(8,128)(2,1)S(1)} %get-tuple-element.75), channel_id=1, source_target_pairs={{0,4},{2,6},{4,0},{6,2},{1,5},{3,7},{5,1},{7,3},{8,12},{10,14},{12... | collective-permute-start | bytes 393224 | tf_op jit(solution)/shard_map/ppermute | solution.py:21
  135.5 1.6 %collective-permute-start.36 = (bf16[4,16,512]{2,1,0:T(8,128)(2,1)S(1)}, bf16[4,16,512]{2,1,0:T(8,128)(2,1)S(1)}, u32[]{:S(2)}, u32[]{:S(2)}) collective-permute-start(bf16[4,16,512]{2,1,0:T(8,128)(2,1)S(1)} %get-tuple-element.69), channel_id=1, source_target_pairs={{0,128},{64,192},{128,0},{192,64},{1,129},{65,193},{129,1},{193,65... | collective-permute-start | bytes 196616 | tf_op jit(solution)/shard_map/ppermute | solution.py:26
  137.0 1.8 %collective-permute-start.37 = (bf16[4,16,512]{2,1,0:T(8,128)(2,1)S(1)}, bf16[4,16,512]{2,1,0:T(8,128)(2,1)S(1)}, u32[]{:S(2)}, u32[]{:S(2)}) collective-permute-start(bf16[4,16,512]{2,1,0:T(8,128)(2,1)S(1)} %get-tuple-element.70), channel_id=1, source_target_pairs={{0,192},{64,128},{128,64},{192,0},{1,193},{65,129},{129,65},{193,1... | collective-permute-start | bytes 196616 | tf_op jit(solution)/shard_map/ppermute | solution.py:26
  139.0 4.6 %collective-permute-start.47 = (bf16[2,16,512]{2,1,0:T(8,128)(2,1)S(1)}, bf16[2,16,512]{2,1,0:T(8,128)(2,1)S(1)}, u32[]{:S(2)}, u32[]{:S(2)}) collective-permute-start(bf16[2,16,512]{2,1,0:T(8,128)(2,1)S(1)} %get-tuple-element.77), channel_id=1, source_target_pairs={{0,1},{1,0},{2,3},{3,2},{4,5},{5,4},{6,7},{7,6},{8,9},{9,8},{10,11... | collective-permute-start | bytes 98312 | tf_op jit(solution)/shard_map/ppermute | solution.py:31
  143.6 1.5 collective-permute-start.49
  146.9 4.0 %collective-permute-done.49.refs_11_ = bf16[2,16,512]{2,1,0:T(8,128)(2,1)S(1)} collective-permute-done((bf16[2,16,512]{2,1,0:T(8,128)(2,1)S(1)}, bf16[2,16,512]{2,1,0:T(8,128)(2,1)S(1)}, u32[]{:S(2)}, u32[]{:S(2)}) %collective-permute-start.49) | collective-permute-done | bytes 32800 | tf_op jit(solution)/shard_map/ppermute | solution.py:31
  150.8 1.3 finished.3
  (90 shorter events, 18.0 us)
Async XLA Ops:
  4.3 38.4 %collective-permute-start.19 = (bf16[2048,512]{1,0:T(8,128)(2,1)S(1)}, bf16[2048,512]{1,0:T(8,128)(2,1)S(1)}, u32[]{:S(2)}, u32[]{:S(2)}) collective-permute-start(bf16[2048,512]{1,0:T(8,128)(2,1)S(1)} %mask_tile.3.refs_4_), channel_id=1, source_target_pairs={{0,8},{8,0},{1,9},{9,1},{2,10},{10,2},{3,11},{11,3},{4,12},{12,4},... | collective-permute-start | bytes 6291464 | tf_op jit(solution)/shard_map/ppermute | solution.py:31
  5.7 42.4 %collective-permute-start.6 = (bf16[512,2048]{1,0:T(8,128)(2,1)S(1)}, bf16[512,2048]{1,0:T(8,128)(2,1)S(1)}, u32[]{:S(2)}, u32[]{:S(2)}) collective-permute-start(bf16[512,2048]{1,0:T(8,128)(2,1)S(1)} %mask_tile.2.refs_4_), channel_id=1, source_target_pairs={{0,8},{8,0},{1,9},{9,1},{2,10},{10,2},{3,11},{11,3},{4,12},{12,4},... | collective-permute-start | bytes 6291464 | tf_op jit(solution)/shard_map/ppermute | solution.py:31
  6.3 7.5 %collective-permute-start.15 = (bf16[4,16,512]{2,1,0:T(8,128)(2,1)S(1)}, bf16[4,16,512]{2,1,0:T(8,128)(2,1)S(1)}, u32[]{:S(2)}, u32[]{:S(2)}) collective-permute-start(bf16[4,16,512]{2,1,0:T(8,128)(2,1)S(1)} %get-tuple-element.51.refs_0_), channel_id=1, source_target_pairs={{0,192},{64,128},{128,64},{192,0},{1,193},{65,129},{129,65},{193,1... | collective-permute-start | bytes 196616 | tf_op jit(solution)/shard_map/ppermute | solution.py:26
  11.0 9.4 %collective-permute-start.14 = (bf16[4,16,512]{2,1,0:T(8,128)(2,1)S(1)}, bf16[4,16,512]{2,1,0:T(8,128)(2,1)S(1)}, u32[]{:S(2)}, u32[]{:S(2)}) collective-permute-start(bf16[4,16,512]{2,1,0:T(8,128)(2,1)S(1)} %get-tuple-element.51.refs_0_), channel_id=1, source_target_pairs={{0,128},{64,192},{128,0},{192,64},{1,129},{65,193},{129,1},{193,65... | collective-permute-start | bytes 196616 | tf_op jit(solution)/shard_map/ppermute | solution.py:26
  11.0 11.1 %collective-permute-start.13 = (bf16[4,16,512]{2,1,0:T(8,128)(2,1)S(1)}, bf16[4,16,512]{2,1,0:T(8,128)(2,1)S(1)}, u32[]{:S(2)}, u32[]{:S(2)}) collective-permute-start(bf16[4,16,512]{2,1,0:T(8,128)(2,1)S(1)} %get-tuple-element.51.refs_0_), channel_id=1, source_target_pairs={{0,64},{64,0},{128,192},{192,128},{1,65},{65,1},{129,193},{193,129... | collective-permute-start | bytes 196616 | tf_op jit(solution)/shard_map/ppermute | solution.py:26
  13.8 8.8 %collective-permute-start.1 = (bf16[2,16,512]{2,1,0:T(8,128)(2,1)S(1)}, bf16[2,16,512]{2,1,0:T(8,128)(2,1)S(1)}, u32[]{:S(2)}, u32[]{:S(2)}) collective-permute-start(bf16[2,16,512]{2,1,0:T(8,128)(2,1)S(1)} %get-tuple-element.41.refs_0_), channel_id=1, source_target_pairs={{0,1},{1,0},{2,3},{3,2},{4,5},{5,4},{6,7},{7,6},{8,9},{9,8},{10,11... | collective-permute-start | bytes 98312 | tf_op jit(solution)/shard_map/ppermute | solution.py:31
  20.4 7.2 %collective-permute-start.2 = (bf16[2,16,512]{2,1,0:T(8,128)(2,1)S(1)}, bf16[2,16,512]{2,1,0:T(8,128)(2,1)S(1)}, u32[]{:S(2)}, u32[]{:S(2)}) collective-permute-start(bf16[2,16,512]{2,1,0:T(8,128)(2,1)S(1)} %get-tuple-element.42), channel_id=1, source_target_pairs={{0,9},{1,8},{8,1},{9,0},{2,11},{3,10},{10,3},{11,2},{4,13},{5,12},... | collective-permute-start | bytes 98312 | tf_op jit(solution)/shard_map/ppermute | solution.py:31
  22.1 8.6 %collective-permute-start = (bf16[2,16,512]{2,1,0:T(8,128)(2,1)S(1)}, bf16[2,16,512]{2,1,0:T(8,128)(2,1)S(1)}, u32[]{:S(2)}, u32[]{:S(2)}) collective-permute-start(bf16[2,16,512]{2,1,0:T(8,128)(2,1)S(1)} %get-tuple-element.42), channel_id=1, source_target_pairs={{0,8},{8,0},{1,9},{9,1},{2,10},{10,2},{3,11},{11,3},{4,12},{12,4},... | collective-permute-start | bytes 98312 | tf_op jit(solution)/shard_map/ppermute | solution.py:31
  22.7 14.2 %collective-permute-start.18 = (bf16[4,4,16,512]{3,2,1,0:T(8,128)(2,1)S(1)}, bf16[4,4,16,512]{3,2,1,0:T(8,128)(2,1)S(1)}, u32[]{:S(2)}, u32[]{:S(2)}) collective-permute-start(bf16[4,4,16,512]{3,2,1,0:T(8,128)(2,1)S(1)} %joined.5.refs_0_), channel_id=1, source_target_pairs={{0,48},{16,0},{32,16},{48,32},{1,49},{17,1},{33,17},{49,33},{2,50}... | collective-permute-start | bytes 786440 | tf_op jit(solution)/shard_map/ppermute | solution.py:21
  27.7 10.6 %collective-permute-start.17 = (bf16[4,4,16,512]{3,2,1,0:T(8,128)(2,1)S(1)}, bf16[4,4,16,512]{3,2,1,0:T(8,128)(2,1)S(1)}, u32[]{:S(2)}, u32[]{:S(2)}) collective-permute-start(bf16[4,4,16,512]{3,2,1,0:T(8,128)(2,1)S(1)} %joined.5.refs_0_), channel_id=1, source_target_pairs={{0,32},{16,48},{32,0},{48,16},{1,33},{17,49},{33,1},{49,17},{2,34}... | collective-permute-start | bytes 786440 | tf_op jit(solution)/shard_map/ppermute | solution.py:21
  30.7 10.4 %collective-permute-start.16 = (bf16[4,4,16,512]{3,2,1,0:T(8,128)(2,1)S(1)}, bf16[4,4,16,512]{3,2,1,0:T(8,128)(2,1)S(1)}, u32[]{:S(2)}, u32[]{:S(2)}) collective-permute-start(bf16[4,4,16,512]{3,2,1,0:T(8,128)(2,1)S(1)} %joined.5.refs_0_), channel_id=1, source_target_pairs={{0,16},{16,32},{32,48},{48,0},{1,17},{17,33},{33,49},{49,1},{2,18}... | collective-permute-start | bytes 786440 | tf_op jit(solution)/shard_map/ppermute | solution.py:21
  36.9 8.4 %collective-permute-start.5 = (bf16[2,2,2,16,512]{4,3,2,1,0:T(8,128)(2,1)S(1)}, bf16[2,2,2,16,512]{4,3,2,1,0:T(8,128)(2,1)S(1)}, u32[]{:S(2)}, u32[]{:S(2)}) collective-permute-start(bf16[2,2,2,16,512]{4,3,2,1,0:T(8,128)(2,1)S(1)} %bitcast.10), channel_id=1, source_target_pairs={{0,6},{2,0},{4,2},{6,4},{1,7},{3,1},{5,3},{7,5},{8,14},{10,8},{12,... | collective-permute-start | bytes 393224 | tf_op jit(solution)/shard_map/ppermute | solution.py:21
  38.3 7.1 %collective-permute-start.4 = (bf16[2,2,2,16,512]{4,3,2,1,0:T(8,128)(2,1)S(1)}, bf16[2,2,2,16,512]{4,3,2,1,0:T(8,128)(2,1)S(1)}, u32[]{:S(2)}, u32[]{:S(2)}) collective-permute-start(bf16[2,2,2,16,512]{4,3,2,1,0:T(8,128)(2,1)S(1)} %bitcast.11), channel_id=1, source_target_pairs={{0,4},{2,6},{4,0},{6,2},{1,5},{3,7},{5,1},{7,3},{8,12},{10,14},{12... | collective-permute-start | bytes 393224 | tf_op jit(solution)/shard_map/ppermute | solution.py:21
  41.1 7.1 %collective-permute-start.3 = (bf16[2,2,2,16,512]{4,3,2,1,0:T(8,128)(2,1)S(1)}, bf16[2,2,2,16,512]{4,3,2,1,0:T(8,128)(2,1)S(1)}, u32[]{:S(2)}, u32[]{:S(2)}) collective-permute-start(bf16[2,2,2,16,512]{4,3,2,1,0:T(8,128)(2,1)S(1)} %bitcast.12), channel_id=1, source_target_pairs={{0,2},{2,4},{4,6},{6,0},{1,3},{3,5},{5,7},{7,1},{8,10},{10,12},{12... | collective-permute-start | bytes 393224 | tf_op jit(solution)/shard_map/ppermute | solution.py:21
  44.0 12.9 %collective-permute-start.20 = (f32[2,2,2,16,512]{4,3,2,1,0:T(8,128)S(1)}, f32[2,2,2,16,512]{4,3,2,1,0:T(8,128)S(1)}, u32[]{:S(2)}, u32[]{:S(2)}) collective-permute-start(f32[2,2,2,16,512]{4,3,2,1,0:T(8,128)S(1)} %get-tuple-element.53), channel_id=1, source_target_pairs={{0,2},{2,4},{4,6},{6,0},{1,3},{3,5},{5,7},{7,1},{8,10},{10,12},{12... | collective-permute-start | bytes 786440 | tf_op jit(solution)/shard_map/ppermute | solution.py:21
  50.0 20.7 %collective-permute-start.7 = (f32[4,4,16,512]{3,2,1,0:T(8,128)S(1)}, f32[4,4,16,512]{3,2,1,0:T(8,128)S(1)}, u32[]{:S(2)}, u32[]{:S(2)}) collective-permute-start(f32[4,4,16,512]{3,2,1,0:T(8,128)S(1)} %get-tuple-element.44), channel_id=1, source_target_pairs={{0,16},{16,32},{32,48},{48,0},{1,17},{17,33},{33,49},{49,1},{2,18}... | collective-permute-start | bytes 1572872 | tf_op jit(solution)/shard_map/ppermute | solution.py:21
  51.8 20.8 %collective-permute-start.8 = (f32[4,4,16,512]{3,2,1,0:T(8,128)S(1)}, f32[4,4,16,512]{3,2,1,0:T(8,128)S(1)}, u32[]{:S(2)}, u32[]{:S(2)}) collective-permute-start(f32[4,4,16,512]{3,2,1,0:T(8,128)S(1)} %get-tuple-element.45), channel_id=1, source_target_pairs={{0,48},{16,0},{32,16},{48,32},{1,49},{17,1},{33,17},{49,33},{2,50}... | collective-permute-start | bytes 1572872 | tf_op jit(solution)/shard_map/ppermute | solution.py:21
  53.9 20.3 %collective-permute-start.9 = (f32[4,4,16,512]{3,2,1,0:T(8,128)S(1)}, f32[4,4,16,512]{3,2,1,0:T(8,128)S(1)}, u32[]{:S(2)}, u32[]{:S(2)}) collective-permute-start(f32[4,4,16,512]{3,2,1,0:T(8,128)S(1)} %get-tuple-element.46), channel_id=1, source_target_pairs={{0,32},{16,48},{32,0},{48,16},{1,33},{17,49},{33,1},{49,17},{2,34}... | collective-permute-start | bytes 1572872 | tf_op jit(solution)/shard_map/ppermute | solution.py:21
  55.1 8.9 %collective-permute-start.21 = (f32[2,2,2,16,512]{4,3,2,1,0:T(8,128)S(1)}, f32[2,2,2,16,512]{4,3,2,1,0:T(8,128)S(1)}, u32[]{:S(2)}, u32[]{:S(2)}) collective-permute-start(f32[2,2,2,16,512]{4,3,2,1,0:T(8,128)S(1)} %get-tuple-element.54), channel_id=1, source_target_pairs={{0,6},{2,0},{4,2},{6,4},{1,7},{3,1},{5,3},{7,5},{8,14},{10,8},{12,... | collective-permute-start | bytes 786440 | tf_op jit(solution)/shard_map/ppermute | solution.py:21
  56.9 9.9 %collective-permute-start.22 = (f32[2,2,2,16,512]{4,3,2,1,0:T(8,128)S(1)}, f32[2,2,2,16,512]{4,3,2,1,0:T(8,128)S(1)}, u32[]{:S(2)}, u32[]{:S(2)}) collective-permute-start(f32[2,2,2,16,512]{4,3,2,1,0:T(8,128)S(1)} %get-tuple-element.55), channel_id=1, source_target_pairs={{0,4},{2,6},{4,0},{6,2},{1,5},{3,7},{5,1},{7,3},{8,12},{10,14},{12... | collective-permute-start | bytes 786440 | tf_op jit(solution)/shard_map/ppermute | solution.py:21
  66.9 11.9 %collective-permute-start.23 = (f32[2,16,512]{2,1,0:T(8,128)S(1)}, f32[2,16,512]{2,1,0:T(8,128)S(1)}, u32[]{:S(2)}, u32[]{:S(2)}) collective-permute-start(f32[2,16,512]{2,1,0:T(8,128)S(1)} %get-tuple-element.57), channel_id=1, source_target_pairs={{0,1},{1,0},{2,3},{3,2},{4,5},{5,4},{6,7},{7,6},{8,9},{9,8},{10,11... | collective-permute-start | bytes 196616 | tf_op jit(solution)/shard_map/ppermute | solution.py:31
  74.3 12.9 %collective-permute-start.10 = (f32[4,16,512]{2,1,0:T(8,128)S(1)}, f32[4,16,512]{2,1,0:T(8,128)S(1)}, u32[]{:S(2)}, u32[]{:S(2)}) collective-permute-start(f32[4,16,512]{2,1,0:T(8,128)S(1)} %get-tuple-element.48), channel_id=1, source_target_pairs={{0,64},{64,0},{128,192},{192,128},{1,65},{65,1},{129,193},{193,129... | collective-permute-start | bytes 393224 | tf_op jit(solution)/shard_map/ppermute | solution.py:26
  74.4 12.8 %collective-permute-start.11 = (f32[4,16,512]{2,1,0:T(8,128)S(1)}, f32[4,16,512]{2,1,0:T(8,128)S(1)}, u32[]{:S(2)}, u32[]{:S(2)}) collective-permute-start(f32[4,16,512]{2,1,0:T(8,128)S(1)} %get-tuple-element.49), channel_id=1, source_target_pairs={{0,128},{64,192},{128,0},{192,64},{1,129},{65,193},{129,1},{193,65... | collective-permute-start | bytes 393224 | tf_op jit(solution)/shard_map/ppermute | solution.py:26
  75.1 12.1 %collective-permute-start.12 = (f32[4,16,512]{2,1,0:T(8,128)S(1)}, f32[4,16,512]{2,1,0:T(8,128)S(1)}, u32[]{:S(2)}, u32[]{:S(2)}) collective-permute-start(f32[4,16,512]{2,1,0:T(8,128)S(1)} %get-tuple-element.50), channel_id=1, source_target_pairs={{0,192},{64,128},{128,64},{192,0},{1,193},{65,129},{129,65},{193,1... | collective-permute-start | bytes 393224 | tf_op jit(solution)/shard_map/ppermute | solution.py:26
  78.8 5.1 %collective-permute-start.24 = (f32[2,16,512]{2,1,0:T(8,128)S(1)}, f32[2,16,512]{2,1,0:T(8,128)S(1)}, u32[]{:S(2)}, u32[]{:S(2)}) collective-permute-start(f32[2,16,512]{2,1,0:T(8,128)S(1)} %get-tuple-element.58), channel_id=1, source_target_pairs={{0,8},{8,0},{1,9},{9,1},{2,10},{10,2},{3,11},{11,3},{4,12},{12,4},... | collective-permute-start | bytes 196616 | tf_op jit(solution)/shard_map/ppermute | solution.py:31
  78.8 8.4 %collective-permute-start.25 = (f32[2,16,512]{2,1,0:T(8,128)S(1)}, f32[2,16,512]{2,1,0:T(8,128)S(1)}, u32[]{:S(2)}, u32[]{:S(2)}) collective-permute-start(f32[2,16,512]{2,1,0:T(8,128)S(1)} %get-tuple-element.59), channel_id=1, source_target_pairs={{0,9},{1,8},{8,1},{9,0},{2,11},{3,10},{10,3},{11,2},{4,13},{5,12},... | collective-permute-start | bytes 196616 | tf_op jit(solution)/shard_map/ppermute | solution.py:31
  87.9 11.2 %collective-permute-start.40 = (bf16[4,16,512]{2,1,0:T(8,128)(2,1)S(1)}, bf16[4,16,512]{2,1,0:T(8,128)(2,1)S(1)}, u32[]{:S(2)}, u32[]{:S(2)}) collective-permute-start(bf16[4,16,512]{2,1,0:T(8,128)(2,1)S(1)} %get-tuple-element.71.refs_0_), channel_id=1, source_target_pairs={{0,192},{64,128},{128,64},{192,0},{1,193},{65,129},{129,65},{193,1... | collective-permute-start | bytes 196616 | tf_op jit(solution)/shard_map/ppermute | solution.py:26
  89.1 10.0 %collective-permute-start.39 = (bf16[4,16,512]{2,1,0:T(8,128)(2,1)S(1)}, bf16[4,16,512]{2,1,0:T(8,128)(2,1)S(1)}, u32[]{:S(2)}, u32[]{:S(2)}) collective-permute-start(bf16[4,16,512]{2,1,0:T(8,128)(2,1)S(1)} %get-tuple-element.71.refs_0_), channel_id=1, source_target_pairs={{0,128},{64,192},{128,0},{192,64},{1,129},{65,193},{129,1},{193,65... | collective-permute-start | bytes 196616 | tf_op jit(solution)/shard_map/ppermute | solution.py:26
  89.2 9.9 %collective-permute-start.38 = (bf16[4,16,512]{2,1,0:T(8,128)(2,1)S(1)}, bf16[4,16,512]{2,1,0:T(8,128)(2,1)S(1)}, u32[]{:S(2)}, u32[]{:S(2)}) collective-permute-start(bf16[4,16,512]{2,1,0:T(8,128)(2,1)S(1)} %get-tuple-element.71.refs_0_), channel_id=1, source_target_pairs={{0,64},{64,0},{128,192},{192,128},{1,65},{65,1},{129,193},{193,129... | collective-permute-start | bytes 196616 | tf_op jit(solution)/shard_map/ppermute | solution.py:26
  92.4 9.5 %collective-permute-start.27 = (bf16[2,16,512]{2,1,0:T(8,128)(2,1)S(1)}, bf16[2,16,512]{2,1,0:T(8,128)(2,1)S(1)}, u32[]{:S(2)}, u32[]{:S(2)}) collective-permute-start(bf16[2,16,512]{2,1,0:T(8,128)(2,1)S(1)} %get-tuple-element.61.refs_0_), channel_id=1, source_target_pairs={{0,1},{1,0},{2,3},{3,2},{4,5},{5,4},{6,7},{7,6},{8,9},{9,8},{10,11... | collective-permute-start | bytes 98312 | tf_op jit(solution)/shard_map/ppermute | solution.py:31
  96.6 7.3 %collective-permute-start.28 = (bf16[2,16,512]{2,1,0:T(8,128)(2,1)S(1)}, bf16[2,16,512]{2,1,0:T(8,128)(2,1)S(1)}, u32[]{:S(2)}, u32[]{:S(2)}) collective-permute-start(bf16[2,16,512]{2,1,0:T(8,128)(2,1)S(1)} %get-tuple-element.62), channel_id=1, source_target_pairs={{0,9},{1,8},{8,1},{9,0},{2,11},{3,10},{10,3},{11,2},{4,13},{5,12},... | collective-permute-start | bytes 98312 | tf_op jit(solution)/shard_map/ppermute | solution.py:31
  99.1 22.2 %collective-permute-start.43 = (bf16[4,4,16,512]{3,2,1,0:T(8,128)(2,1)S(1)}, bf16[4,4,16,512]{3,2,1,0:T(8,128)(2,1)S(1)}, u32[]{:S(2)}, u32[]{:S(2)}) collective-permute-start(bf16[4,4,16,512]{3,2,1,0:T(8,128)(2,1)S(1)} %joined.7.refs_0_), channel_id=1, source_target_pairs={{0,48},{16,0},{32,16},{48,32},{1,49},{17,1},{33,17},{49,33},{2,50}... | collective-permute-start | bytes 786440 | tf_op jit(solution)/shard_map/ppermute | solution.py:21
  104.0 8.2 %collective-permute-start.31 = (bf16[2,2,2,16,512]{4,3,2,1,0:T(8,128)(2,1)S(1)}, bf16[2,2,2,16,512]{4,3,2,1,0:T(8,128)(2,1)S(1)}, u32[]{:S(2)}, u32[]{:S(2)}) collective-permute-start(bf16[2,2,2,16,512]{4,3,2,1,0:T(8,128)(2,1)S(1)} %bitcast.14), channel_id=1, source_target_pairs={{0,6},{2,0},{4,2},{6,4},{1,7},{3,1},{5,3},{7,5},{8,14},{10,8},{12,... | collective-permute-start | bytes 393224 | tf_op jit(solution)/shard_map/ppermute | solution.py:21
  109.6 6.5 %collective-permute-start.30 = (bf16[2,2,2,16,512]{4,3,2,1,0:T(8,128)(2,1)S(1)}, bf16[2,2,2,16,512]{4,3,2,1,0:T(8,128)(2,1)S(1)}, u32[]{:S(2)}, u32[]{:S(2)}) collective-permute-start(bf16[2,2,2,16,512]{4,3,2,1,0:T(8,128)(2,1)S(1)} %bitcast.15), channel_id=1, source_target_pairs={{0,4},{2,6},{4,0},{6,2},{1,5},{3,7},{5,1},{7,3},{8,12},{10,14},{12... | collective-permute-start | bytes 393224 | tf_op jit(solution)/shard_map/ppermute | solution.py:21
  109.6 6.5 %collective-permute-start.29 = (bf16[2,2,2,16,512]{4,3,2,1,0:T(8,128)(2,1)S(1)}, bf16[2,2,2,16,512]{4,3,2,1,0:T(8,128)(2,1)S(1)}, u32[]{:S(2)}, u32[]{:S(2)}) collective-permute-start(bf16[2,2,2,16,512]{4,3,2,1,0:T(8,128)(2,1)S(1)} %bitcast.16), channel_id=1, source_target_pairs={{0,2},{2,4},{4,6},{6,0},{1,3},{3,5},{5,7},{7,1},{8,10},{10,12},{12... | collective-permute-start | bytes 393224 | tf_op jit(solution)/shard_map/ppermute | solution.py:21
  111.1 10.7 %collective-permute-start.42 = (bf16[4,4,16,512]{3,2,1,0:T(8,128)(2,1)S(1)}, bf16[4,4,16,512]{3,2,1,0:T(8,128)(2,1)S(1)}, u32[]{:S(2)}, u32[]{:S(2)}) collective-permute-start(bf16[4,4,16,512]{3,2,1,0:T(8,128)(2,1)S(1)} %joined.7.refs_0_), channel_id=1, source_target_pairs={{0,32},{16,48},{32,0},{48,16},{1,33},{17,49},{33,1},{49,17},{2,34}... | collective-permute-start | bytes 786440 | tf_op jit(solution)/shard_map/ppermute | solution.py:21
  112.1 13.5 %collective-permute-start.41 = (bf16[4,4,16,512]{3,2,1,0:T(8,128)(2,1)S(1)}, bf16[4,4,16,512]{3,2,1,0:T(8,128)(2,1)S(1)}, u32[]{:S(2)}, u32[]{:S(2)}) collective-permute-start(bf16[4,4,16,512]{3,2,1,0:T(8,128)(2,1)S(1)} %joined.7.refs_0_), channel_id=1, source_target_pairs={{0,16},{16,32},{32,48},{48,0},{1,17},{17,33},{33,49},{49,1},{2,18}... | collective-permute-start | bytes 786440 | tf_op jit(solution)/shard_map/ppermute | solution.py:21
  118.0 13.5 %collective-permute-start.32 = (bf16[4,4,16,512]{3,2,1,0:T(8,128)(2,1)S(1)}, bf16[4,4,16,512]{3,2,1,0:T(8,128)(2,1)S(1)}, u32[]{:S(2)}, u32[]{:S(2)}) collective-permute-start(bf16[4,4,16,512]{3,2,1,0:T(8,128)(2,1)S(1)} %get-tuple-element.64), channel_id=1, source_target_pairs={{0,16},{16,32},{32,48},{48,0},{1,17},{17,33},{33,49},{49,1},{2,18}... | collective-permute-start | bytes 786440 | tf_op jit(solution)/shard_map/ppermute | solution.py:21
  118.1 15.3 %collective-permute-start.33 = (bf16[4,4,16,512]{3,2,1,0:T(8,128)(2,1)S(1)}, bf16[4,4,16,512]{3,2,1,0:T(8,128)(2,1)S(1)}, u32[]{:S(2)}, u32[]{:S(2)}) collective-permute-start(bf16[4,4,16,512]{3,2,1,0:T(8,128)(2,1)S(1)} %get-tuple-element.65), channel_id=1, source_target_pairs={{0,48},{16,0},{32,16},{48,32},{1,49},{17,1},{33,17},{49,33},{2,50}... | collective-permute-start | bytes 786440 | tf_op jit(solution)/shard_map/ppermute | solution.py:21
  121.3 13.0 %collective-permute-start.34 = (bf16[4,4,16,512]{3,2,1,0:T(8,128)(2,1)S(1)}, bf16[4,4,16,512]{3,2,1,0:T(8,128)(2,1)S(1)}, u32[]{:S(2)}, u32[]{:S(2)}) collective-permute-start(bf16[4,4,16,512]{3,2,1,0:T(8,128)(2,1)S(1)} %get-tuple-element.66), channel_id=1, source_target_pairs={{0,32},{16,48},{32,0},{48,16},{1,33},{17,49},{33,1},{49,17},{2,34}... | collective-permute-start | bytes 786440 | tf_op jit(solution)/shard_map/ppermute | solution.py:21
  127.0 10.1 %collective-permute-start.44 = (bf16[2,2,2,16,512]{4,3,2,1,0:T(8,128)(2,1)S(1)}, bf16[2,2,2,16,512]{4,3,2,1,0:T(8,128)(2,1)S(1)}, u32[]{:S(2)}, u32[]{:S(2)}) collective-permute-start(bf16[2,2,2,16,512]{4,3,2,1,0:T(8,128)(2,1)S(1)} %get-tuple-element.73), channel_id=1, source_target_pairs={{0,2},{2,4},{4,6},{6,0},{1,3},{3,5},{5,7},{7,1},{8,10},{10,12},{12... | collective-permute-start | bytes 393224 | tf_op jit(solution)/shard_map/ppermute | solution.py:21
  130.1 8.8 %collective-permute-start.45 = (bf16[2,2,2,16,512]{4,3,2,1,0:T(8,128)(2,1)S(1)}, bf16[2,2,2,16,512]{4,3,2,1,0:T(8,128)(2,1)S(1)}, u32[]{:S(2)}, u32[]{:S(2)}) collective-permute-start(bf16[2,2,2,16,512]{4,3,2,1,0:T(8,128)(2,1)S(1)} %get-tuple-element.74), channel_id=1, source_target_pairs={{0,6},{2,0},{4,2},{6,4},{1,7},{3,1},{5,3},{7,5},{8,14},{10,8},{12,... | collective-permute-start | bytes 393224 | tf_op jit(solution)/shard_map/ppermute | solution.py:21
  131.4 7.5 %collective-permute-start.46 = (bf16[2,2,2,16,512]{4,3,2,1,0:T(8,128)(2,1)S(1)}, bf16[2,2,2,16,512]{4,3,2,1,0:T(8,128)(2,1)S(1)}, u32[]{:S(2)}, u32[]{:S(2)}) collective-permute-start(bf16[2,2,2,16,512]{4,3,2,1,0:T(8,128)(2,1)S(1)} %get-tuple-element.75), channel_id=1, source_target_pairs={{0,4},{2,6},{4,0},{6,2},{1,5},{3,7},{5,1},{7,3},{8,12},{10,14},{12... | collective-permute-start | bytes 393224 | tf_op jit(solution)/shard_map/ppermute | solution.py:21
  134.4 9.2 %collective-permute-start.35 = (bf16[4,16,512]{2,1,0:T(8,128)(2,1)S(1)}, bf16[4,16,512]{2,1,0:T(8,128)(2,1)S(1)}, u32[]{:S(2)}, u32[]{:S(2)}) collective-permute-start(bf16[4,16,512]{2,1,0:T(8,128)(2,1)S(1)} %get-tuple-element.68), channel_id=1, source_target_pairs={{0,64},{64,0},{128,192},{192,128},{1,65},{65,1},{129,193},{193,129... | collective-permute-start | bytes 196616 | tf_op jit(solution)/shard_map/ppermute | solution.py:26
  135.5 10.4 %collective-permute-start.36 = (bf16[4,16,512]{2,1,0:T(8,128)(2,1)S(1)}, bf16[4,16,512]{2,1,0:T(8,128)(2,1)S(1)}, u32[]{:S(2)}, u32[]{:S(2)}) collective-permute-start(bf16[4,16,512]{2,1,0:T(8,128)(2,1)S(1)} %get-tuple-element.69), channel_id=1, source_target_pairs={{0,128},{64,192},{128,0},{192,64},{1,129},{65,193},{129,1},{193,65... | collective-permute-start | bytes 196616 | tf_op jit(solution)/shard_map/ppermute | solution.py:26
  137.0 8.8 %collective-permute-start.37 = (bf16[4,16,512]{2,1,0:T(8,128)(2,1)S(1)}, bf16[4,16,512]{2,1,0:T(8,128)(2,1)S(1)}, u32[]{:S(2)}, u32[]{:S(2)}) collective-permute-start(bf16[4,16,512]{2,1,0:T(8,128)(2,1)S(1)} %get-tuple-element.70), channel_id=1, source_target_pairs={{0,192},{64,128},{128,64},{192,0},{1,193},{65,129},{129,65},{193,1... | collective-permute-start | bytes 196616 | tf_op jit(solution)/shard_map/ppermute | solution.py:26
  139.0 7.9 %collective-permute-start.47 = (bf16[2,16,512]{2,1,0:T(8,128)(2,1)S(1)}, bf16[2,16,512]{2,1,0:T(8,128)(2,1)S(1)}, u32[]{:S(2)}, u32[]{:S(2)}) collective-permute-start(bf16[2,16,512]{2,1,0:T(8,128)(2,1)S(1)} %get-tuple-element.77), channel_id=1, source_target_pairs={{0,1},{1,0},{2,3},{3,2},{4,5},{5,4},{6,7},{7,6},{8,9},{9,8},{10,11... | collective-permute-start | bytes 98312 | tf_op jit(solution)/shard_map/ppermute | solution.py:31
  143.6 7.2 %collective-permute-start.49 = (bf16[2,16,512]{2,1,0:T(8,128)(2,1)S(1)}, bf16[2,16,512]{2,1,0:T(8,128)(2,1)S(1)}, u32[]{:S(2)}, u32[]{:S(2)}) collective-permute-start(bf16[2,16,512]{2,1,0:T(8,128)(2,1)S(1)} %get-tuple-element.79), channel_id=1, source_target_pairs={{0,9},{1,8},{8,1},{9,0},{2,11},{3,10},{10,3},{11,2},{4,13},{5,12},... | collective-permute-start | bytes 98312 | tf_op jit(solution)/shard_map/ppermute | solution.py:31
  (12 other events, 201.5 us)
where the time goes:
time: 154 us; the launch traced here: 152 us
  starting transfers between devices  91.5 us (59%)
  waiting for transfers between devices  45.1 us (29%)
  Pallas kernels  11.4 us (7%)
  local copies, waits for them, and re-layouts  3.19 us (2%)
    ppermute x24, starting transfers between devices, shifted(): return lax.ppermute(x, axis, [(i, (i + step) % n) for i in range(n)])  41.5 us
    ppermute x14, starting transfers between devices, swapped(): return lax.ppermute(x, axes, [(i, n - 1 - i) for i in range(n)])  31.2 us
    ppermute x24, waiting for transfers between devices, shifted(): return lax.ppermute(x, axis, [(i, (i + step) % n) for i in range(n)])  30.5 us
    ppermute x12, starting transfers between devices, flipped(): return lax.ppermute(x, axis, [(i, i ^ mask) for i in range(n)])  18.8 us
    ppermute x14, waiting for transfers between devices, swapped(): return lax.ppermute(x, axes, [(i, n - 1 - i) for i in range(n)])  12.4 us
    pallas_call x2, Pallas kernels, cols_product(): pl.pallas_call(kernel, out_shape=[sds(shape, F32 if s == 0 else wire) for...  3.76 us
    unnamed x21, local copies, waits for them, and re-layouts  3.19 us
  transfers between devices with their start and end apart: 50, of which 19 were waited for; matrix products, arithmetic and copies ran while one was open for 1% of the time, Pallas kernels for 5%

commit v1 on v0

--- a/solution.py
+++ b/solution.py
@@ -56,18 +56,18 @@
     edge_c = tile.shape[1] // cols
 
     def kernel(mask_ref, tile_ref, out_ref):
-        p = pl.program_id(0)
-        start = pl.multiple_of(p * edge_r, edge_r)
-        for q in range(cols):
-            cut = pl.ds(q * edge_c, edge_c)
-            value = mask_ref[q, p] if turned else mask_ref[p, q]
-            out_ref[pl.ds(start, edge_r), cut] = tile_ref[:, cut] * value.astype(F32).astype(BF16)
-
-    return pl.pallas_call(
-        kernel,
-        grid=(rows,),
+        @pl.loop(0, rows)
+        def _(p):
+            down = pl.ds(pl.multiple_of(p * edge_r, edge_r), edge_r)
+            for q in range(cols):
+                cut = pl.ds(q * edge_c, edge_c)
+                value = mask_ref[q, p] if turned else mask_ref[p, q]
+                out_ref[down, cut] = tile_ref[down, cut] * value.astype(F32).astype(BF16)
+
+    return pl.pallas_call(
+        kernel,
         out_shape=sds(tile.shape, tile.dtype),
-        in_specs=smem(1) + [pl.BlockSpec((edge_r, tile.shape[1]), lambda p: (p, 0))],
+        in_specs=smem(1) + vmem(1),
         out_specs=vmem(1)[0],
         compiler_params=LIMIT,
         name="mask_tile",
@@ -139,7 +139,7 @@
     )(*on_chip(*parts, *tiles))
 
 
-def cols_product(parts, tiles, transposed, wire):
+def cols_product(parts, tiles, transposed, wire, far):
     i_count, d_count = parts[0].shape[-2:]
     cuts = (tiles[0].shape[0] if transposed else tiles[0].shape[1]) // d_count
 
@@ -173,7 +173,7 @@
     shape = (4, cuts, i_count, d_count)
     return pl.pallas_call(
         kernel,
-        out_shape=[sds(shape, F32 if s == 0 else wire) for s in range(4)],
+        out_shape=[sds(shape, (F32, wire, far, wire)[s]) for s in range(4)],
         in_specs=vmem(6),
         out_specs=vmem(4),
         scratch_shapes=[pltpu.VMEM((2, 16, i_count, d_count), BF16)],
@@ -239,7 +239,7 @@
                 for ref in wholes[1:]:
                     total = total + ref[r].astype(F32)
                 for ref in halves[k]:
-                    total = total + ref[half].astype(F32)
+                    total = total + ref[0, half].astype(F32)
                 if n_base:
                     total = total + stage[r]
                 place_j, place_a = (cols * r_count + r, wide) if swap else (wide, cols * r_count + r)
@@ -284,7 +284,7 @@
         out_specs=vmem(3),
         compiler_params=LIMIT,
         name="prepared",
-    )(*on_chip(amps))
+    )(amps)
 
 
 def wide_gather(piece):
@@ -296,23 +296,59 @@
 
 
 def cols_gather(near, far):
-    zh = swapped(near, ("zh",))
-    both = swapped(far, ("core", "zh"))
-    core = swapped(far, ("core",))
-    parts = joined([near, core, zh, both])
-    parts = parts.reshape(2, 2, *parts.shape[1:])
+    half = joined([near, swapped(far, ("core",))])
+    parts = joined([half, swapped(half, ("zh",))])
     here = {0: parts}
     for s in SHIFTS:
         here[s] = shifted(parts, "y", s)
     return [here[s] for s in range(4)]
 
 
+def split_sum(arrays):
+    inside = (arrays[0].shape[0], *arrays[0].shape[2:])
+
+    def kernel(*refs):
+        ins, outs = refs[:-2], refs[-2:]
+        for flip in range(inside[0]):
+            for q in range(2):
+                total = ins[0][flip, q].astype(F32)
+                for ref in ins[1:]:
+                    total = total + ref[flip, q].astype(F32)
+                outs[q][flip] = total.astype(outs[q].dtype)
+
+    return pl.pallas_call(
+        kernel,
+        out_shape=[sds(inside, F32)] * 2,
+        in_specs=vmem(len(arrays)),
+        out_specs=vmem(2),
+        compiler_params=LIMIT,
+        name="split_sum",
+    )(*on_chip(*arrays))
+
+
+def woven(near, far, wire):
+    _, count, i_count, n_cols = near.shape
+
+    def kernel(near_ref, far_ref, out_ref):
+        core = lax.axis_index("core")
+        for half in range(count):
+            out_ref[half * 2 + core] = near_ref[1, half].astype(out_ref.dtype)
+            out_ref[half * 2 + (core ^ 1)] = far_ref[1, half].astype(out_ref.dtype)
+
+    return pl.pallas_call(
+        kernel,
+        out_shape=sds((2 * count, i_count, n_cols), wire),
+        in_specs=vmem(2),
+        out_specs=vmem(1)[0],
+        compiler_params=LIMIT,
+        name="woven",
+    )(*on_chip(near, far))
+
+
 def cols_sum(outs, wire):
-    arrays = [outs[0]] + [shifted(outs[s], "y", s) for s in SHIFTS]
-    own, core, zh, both = summed(arrays, wire, 2)
-    near = [own, swapped(zh, ("zh",))]
-    far = [swapped(core, ("core",)), swapped(both, ("core", "zh"))]
-    return near, far
+    near, away = split_sum([outs[0]] + [shifted(outs[s], "y", s) for s in SHIFTS])
+    far = swapped(away, ("core",))
+    return swapped(woven(near, far, wire), ("zh",)), [near], [far]
 
 
 def wide_sum(outs, wire):
@@ -324,11 +360,11 @@
 def sweep(piece, near, far, wide_tiles, cols_tiles, transposed, wire):
     wide_parts = wide_gather(piece)
     cols_parts = cols_gather(near, far)
-    outs = cols_product(cols_parts, cols_tiles, transposed, wire)
+    outs = cols_product(cols_parts, cols_tiles, transposed, wire, wire)
     whole = wide_sum(outs, wire)
     outs = wide_product(wide_parts, wide_tiles, transposed, wire)
-    near, far = cols_sum(outs, wire)
-    return whole, near, far
+    zh, near, far = cols_sum(outs, wire)
+    return whole + [zh], near, far
 
 
 def body(

time: 154 us -> 162 us (1.052)
  waiting for transfers between devices: 45.1 us -> 73.5 us
  starting transfers between devices: 91.5 us -> 69.6 us
    ppermute x12, waiting for transfers between devices: 2.18 us -> 24.2 us  [flipped(): return lax.ppermute(x, axis, [(i, i ^ mask) for i in range(n)])]
    ppermute x14 -> x10, starting transfers between devices: 31.2 us -> 14.2 us  [swapped(): return lax.ppermute(x, axes, [(i, n - 1 - i) for i in range(n)])]
    ppermute x24, waiting for transfers between devices: 30.5 us -> 36.9 us  [shifted(): return lax.ppermute(x, axis, [(i, (i + step) % n) for i in range(n)])]
    ppermute x24, starting transfers between devices: 41.5 us -> 36.6 us  [shifted(): return lax.ppermute(x, axis, [(i, (i + step) % n) for i in range(n)])]
    pallas_call x4 -> x8, Pallas kernels: 6.32 us -> 6.07 us  [the longest x2 3.76 us: cols_product(): pl.pallas_call(kernel, out_shape=[sds(shape, (F32, wire, far, wire)[s]) f...]
    ppermute x14 -> x10, waiting for transfers between devices: 12.4 us -> 12.5 us  [swapped(): return lax.ppermute(x, axes, [(i, n - 1 - i) for i in range(n)])]
  transfers between devices with their start and end apart: 50 -> 46, of which waited for: 19 -> 25; matrix products, arithmetic and copies ran while one was open for 1% -> 0% of each run, Pallas kernels for 5% -> 5%
where the time goes in v1:
time: 162 us; the launch traced here: 159 us
  waiting for transfers between devices  73.5 us (45%)
  starting transfers between devices  69.6 us (43%)
  Pallas kernels  11.1 us (7%)
  local copies, waits for them, and re-layouts  3.51 us (2%)
    ppermute x24, waiting for transfers between devices, shifted(): return lax.ppermute(x, axis, [(i, (i + step) % n) for i in range(n)])  36.9 us
    ppermute x24, starting transfers between devices, shifted(): return lax.ppermute(x, axis, [(i, (i + step) % n) for i in range(n)])  36.6 us
    ppermute x12, waiting for transfers between devices, flipped(): return lax.ppermute(x, axis, [(i, i ^ mask) for i in range(n)])  24.2 us
    ppermute x12, starting transfers between devices, flipped(): return lax.ppermute(x, axis, [(i, i ^ mask) for i in range(n)])  18.8 us
    ppermute x10, starting transfers between devices, swapped(): return lax.ppermute(x, axes, [(i, n - 1 - i) for i in range(n)])  14.2 us
    ppermute x10, waiting for transfers between devices, swapped(): return lax.ppermute(x, axes, [(i, n - 1 - i) for i in range(n)])  12.5 us
    pallas_call x2, Pallas kernels, cols_product(): pl.pallas_call(kernel, out_shape=[sds(shape, (F32, wire, far, wire)[s]) f...  3.76 us
    unnamed x21, local copies, waits for them, and re-layouts  3.51 us
  transfers between devices with their start and end apart: 46, of which 25 were waited for; matrix products, arithmetic and copies ran while one was open for 0% of the time, Pallas kernels for 5%

profile of v1, /device:TPU:8, one launch (start us, length us, event | category | flops | bytes accessed | tf_op | source)
XLA Modules:
  0.0 158.7 jit_solution(13714374715231937058)
XLA Ops:
  0.6 1.6 copy-done
  5.9 4.7 %collective-permute-start.14 = (bf16[4,16,512]{2,1,0:T(8,128)(2,1)S(1)}, bf16[4,16,512]{2,1,0:T(8,128)(2,1)S(1)}, u32[]{:S(2)}, u32[]{:S(2)}) collective-permute-start(bf16[4,16,512]{2,1,0:T(8,128)(2,1)S(1)} %get-tuple-element.47.refs_0_), channel_id=1, source_target_pairs={{0,192},{64,128},{128,64},{192,0},{1,193},{65,129},{129,65},{193,1... | collective-permute-start | bytes 196616 | tf_op jit(solution)/shard_map/ppermute | solution.py:26
  11.3 2.3 %collective-permute-done.14.refs_3_ = bf16[4,16,512]{2,1,0:T(8,128)(2,1)S(1)} collective-permute-done((bf16[4,16,512]{2,1,0:T(8,128)(2,1)S(1)}, bf16[4,16,512]{2,1,0:T(8,128)(2,1)S(1)}, u32[]{:S(2)}, u32[]{:S(2)}) %collective-permute-start.14) | collective-permute-done | bytes 65568 | tf_op jit(solution)/shard_map/ppermute | solution.py:26
  13.6 2.6 %collective-permute-done.13.refs_2_ = bf16[4,16,512]{2,1,0:T(8,128)(2,1)S(1)} collective-permute-done((bf16[4,16,512]{2,1,0:T(8,128)(2,1)S(1)}, bf16[4,16,512]{2,1,0:T(8,128)(2,1)S(1)}, u32[]{:S(2)}, u32[]{:S(2)}) %collective-permute-start.13) | collective-permute-done | bytes 65568 | tf_op jit(solution)/shard_map/ppermute | solution.py:26
  16.4 2.8 %collective-permute-start.17 = (bf16[4,4,16,512]{3,2,1,0:T(8,128)(2,1)S(1)}, bf16[4,4,16,512]{3,2,1,0:T(8,128)(2,1)S(1)}, u32[]{:S(2)}, u32[]{:S(2)}) collective-permute-start(bf16[4,4,16,512]{3,2,1,0:T(8,128)(2,1)S(1)} %joined.8.refs_0_), channel_id=1, source_target_pairs={{0,48},{16,0},{32,16},{48,32},{1,49},{17,1},{33,17},{49,33},{2,50}... | collective-permute-start | bytes 786440 | tf_op jit(solution)/shard_map/ppermute | solution.py:21
  20.9 9.4 %collective-permute-done.17.refs_3_ = bf16[4,4,16,512]{3,2,1,0:T(8,128)(2,1)S(1)} collective-permute-done((bf16[4,4,16,512]{3,2,1,0:T(8,128)(2,1)S(1)}, bf16[4,4,16,512]{3,2,1,0:T(8,128)(2,1)S(1)}, u32[]{:S(2)}, u32[]{:S(2)}) %collective-permute-start.17) | collective-permute-done | bytes 262176 | tf_op jit(solution)/shard_map/ppermute | solution.py:21
  30.3 6.4 %collective-permute-start.1 = (bf16[2,2,16,512]{3,2,1,0:T(8,128)(2,1)S(1)}, bf16[2,2,16,512]{3,2,1,0:T(8,128)(2,1)S(1)}, u32[]{:S(2)}, u32[]{:S(2)}) collective-permute-start(bf16[2,2,16,512]{3,2,1,0:T(8,128)(2,1)S(1)} %joined.6.refs_0_), channel_id=1, source_target_pairs={{0,1},{1,0},{2,3},{3,2},{4,5},{5,4},{6,7},{7,6},{8,9},{9,8},{10,11... | collective-permute-start | bytes 196616 | tf_op jit(solution)/shard_map/ppermute | solution.py:31
  37.9 1.7 %collective-permute-start.19 = (f32[2,2,2,16,512]{4,3,2,1,0:T(8,128)S(1)}, f32[2,2,2,16,512]{4,3,2,1,0:T(8,128)S(1)}, u32[]{:S(2)}, u32[]{:S(2)}) collective-permute-start(f32[2,2,2,16,512]{4,3,2,1,0:T(8,128)S(1)} %get-tuple-element.49), channel_id=1, source_target_pairs={{0,2},{2,4},{4,6},{6,0},{1,3},{3,5},{5,7},{7,1},{8,10},{10,12},{12... | collective-permute-start | bytes 786440 | tf_op jit(solution)/shard_map/ppermute | solution.py:21
  40.1 2.3 %collective-permute-start.3 = (bf16[2,2,2,16,512]{4,3,2,1,0:T(8,128)(2,1)S(1)}, bf16[2,2,2,16,512]{4,3,2,1,0:T(8,128)(2,1)S(1)}, u32[]{:S(2)}, u32[]{:S(2)}) collective-permute-start(bf16[2,2,2,16,512]{4,3,2,1,0:T(8,128)(2,1)S(1)} %joined.7.refs_0_), channel_id=1, source_target_pairs={{0,4},{2,6},{4,0},{6,2},{1,5},{3,7},{5,1},{7,3},{8,12},{10,14},{12... | collective-permute-start | bytes 393224 | tf_op jit(solution)/shard_map/ppermute | solution.py:21
  42.4 1.4 collective-permute-start.2
  43.9 1.5 collective-permute-done.4.refs_3_
  45.4 1.4 collective-permute-done.3.refs_2_
  46.8 3.5 %collective-permute-done.2.refs_1_ = bf16[2,2,2,16,512]{4,3,2,1,0:T(8,128)(2,1)S(1)} collective-permute-done((bf16[2,2,2,16,512]{4,3,2,1,0:T(8,128)(2,1)S(1)}, bf16[2,2,2,16,512]{4,3,2,1,0:T(8,128)(2,1)S(1)}, u32[]{:S(2)}, u32[]{:S(2)}) %collective-permute-start.2) | collective-permute-done | bytes 131104 | tf_op jit(solution)/shard_map/ppermute | solution.py:21
  50.3 1.8 %cols_product.2 = (f32[4,4,16,512]{3,2,1,0:T(8,128)S(1)}, f32[4,4,16,512]{3,2,1,0:T(8,128)S(1)}, f32[4,4,16,512]{3,2,1,0:T(8,128)S(1)}, f32[4,4,16,512]{3,2,1,0:T(8,128)S(1)}) custom-call(bf16[2,2,2,16,512]{4,3,2,1,0:T(8,128)(2,1)S(1)} %joined.7.refs_0_, bf16[2,2,2,16,512]{4,3,2,1,0:T(8,128)(2,1)S(1)} %collective-permute-done.2.refs_1_, ...), custom_call_target="tpu_custom_call" | custom-call | tf_op jit(solution)/shard_map/cols_product/pallas_call | solution.py:174
  52.3 4.2 %collective-permute-start.7 = (f32[4,4,16,512]{3,2,1,0:T(8,128)S(1)}, f32[4,4,16,512]{3,2,1,0:T(8,128)S(1)}, u32[]{:S(2)}, u32[]{:S(2)}) collective-permute-start(f32[4,4,16,512]{3,2,1,0:T(8,128)S(1)} %get-tuple-element.41), channel_id=1, source_target_pairs={{0,48},{16,0},{32,16},{48,32},{1,49},{17,1},{33,17},{49,33},{2,50}... | collective-permute-start | bytes 1572872 | tf_op jit(solution)/shard_map/ppermute | solution.py:21
  56.5 1.4 collective-permute-start.8
  57.9 1.7 %collective-permute-start.20 = (f32[2,2,2,16,512]{4,3,2,1,0:T(8,128)S(1)}, f32[2,2,2,16,512]{4,3,2,1,0:T(8,128)S(1)}, u32[]{:S(2)}, u32[]{:S(2)}) collective-permute-start(f32[2,2,2,16,512]{4,3,2,1,0:T(8,128)S(1)} %get-tuple-element.50), channel_id=1, source_target_pairs={{0,6},{2,0},{4,2},{6,4},{1,7},{3,1},{5,3},{7,5},{8,14},{10,8},{12,... | collective-permute-start | bytes 786440 | tf_op jit(solution)/shard_map/ppermute | solution.py:21
  60.9 5.8 %collective-permute-done.20.refs_2_ = f32[2,2,2,16,512]{4,3,2,1,0:T(8,128)S(1)} collective-permute-done((f32[2,2,2,16,512]{4,3,2,1,0:T(8,128)S(1)}, f32[2,2,2,16,512]{4,3,2,1,0:T(8,128)S(1)}, u32[]{:S(2)}, u32[]{:S(2)}) %collective-permute-start.20) | collective-permute-done | bytes 262176 | tf_op jit(solution)/shard_map/ppermute | solution.py:21
  66.7 2.8 %collective-permute-done.21.refs_3_ = f32[2,2,2,16,512]{4,3,2,1,0:T(8,128)S(1)} collective-permute-done((f32[2,2,2,16,512]{4,3,2,1,0:T(8,128)S(1)}, f32[2,2,2,16,512]{4,3,2,1,0:T(8,128)S(1)}, u32[]{:S(2)}, u32[]{:S(2)}) %collective-permute-start.21) | collective-permute-done | bytes 262176 | tf_op jit(solution)/shard_map/ppermute | solution.py:21
  69.6 1.3 collective-permute-done.22.far_ref.refs_11_
  71.0 5.5 %collective-permute-start.23 = (f32[4,16,512]{2,1,0:T(8,128)S(1)}, f32[4,16,512]{2,1,0:T(8,128)S(1)}, u32[]{:S(2)}, u32[]{:S(2)}) collective-permute-start(f32[4,16,512]{2,1,0:T(8,128)S(1)} %woven.2), channel_id=1, source_target_pairs={{0,1},{1,0},{2,3},{3,2},{4,5},{5,4},{6,7},{7,6},{8,9},{9,8},{10,11... | collective-permute-start | bytes 393224 | tf_op jit(solution)/shard_map/ppermute | solution.py:31
  76.9 1.8 %collective-permute-done.8.refs_3_ = f32[4,4,16,512]{3,2,1,0:T(8,128)S(1)} collective-permute-done((f32[4,4,16,512]{3,2,1,0:T(8,128)S(1)}, f32[4,4,16,512]{3,2,1,0:T(8,128)S(1)}, u32[]{:S(2)}, u32[]{:S(2)}) %collective-permute-start.8) | collective-permute-done | bytes 524320 | tf_op jit(solution)/shard_map/ppermute | solution.py:21
  79.5 1.8 %collective-permute-start.10 = (f32[4,16,512]{2,1,0:T(8,128)S(1)}, f32[4,16,512]{2,1,0:T(8,128)S(1)}, u32[]{:S(2)}, u32[]{:S(2)}) collective-permute-start(f32[4,16,512]{2,1,0:T(8,128)S(1)} %get-tuple-element.45), channel_id=1, source_target_pairs={{0,128},{64,192},{128,0},{192,64},{1,129},{65,193},{129,1},{193,65... | collective-permute-start | bytes 393224 | tf_op jit(solution)/shard_map/ppermute | solution.py:26
  81.3 1.9 %collective-permute-start.11 = (f32[4,16,512]{2,1,0:T(8,128)S(1)}, f32[4,16,512]{2,1,0:T(8,128)S(1)}, u32[]{:S(2)}, u32[]{:S(2)}) collective-permute-start(f32[4,16,512]{2,1,0:T(8,128)S(1)} %get-tuple-element.46), channel_id=1, source_target_pairs={{0,192},{64,128},{128,64},{192,0},{1,193},{65,129},{129,65},{193,1... | collective-permute-start | bytes 393224 | tf_op jit(solution)/shard_map/ppermute | solution.py:26
  83.3 5.1 %collective-permute-done.9.refs_6_ = f32[4,16,512]{2,1,0:T(8,128)S(1)} collective-permute-done((f32[4,16,512]{2,1,0:T(8,128)S(1)}, f32[4,16,512]{2,1,0:T(8,128)S(1)}, u32[]{:S(2)}, u32[]{:S(2)}) %collective-permute-start.9) | collective-permute-done | bytes 131104 | tf_op jit(solution)/shard_map/ppermute | solution.py:26
  88.4 4.4 %collective-permute-done.10.refs_7_ = f32[4,16,512]{2,1,0:T(8,128)S(1)} collective-permute-done((f32[4,16,512]{2,1,0:T(8,128)S(1)}, f32[4,16,512]{2,1,0:T(8,128)S(1)}, u32[]{:S(2)}, u32[]{:S(2)}) %collective-permute-start.10) | collective-permute-done | bytes 131104 | tf_op jit(solution)/shard_map/ppermute | solution.py:26
  93.5 1.6 collective-permute-start.37
  95.1 2.9 %collective-permute-start.36 = (bf16[4,16,512]{2,1,0:T(8,128)(2,1)S(1)}, bf16[4,16,512]{2,1,0:T(8,128)(2,1)S(1)}, u32[]{:S(2)}, u32[]{:S(2)}) collective-permute-start(bf16[4,16,512]{2,1,0:T(8,128)(2,1)S(1)} %get-tuple-element.65.refs_0_), channel_id=1, source_target_pairs={{0,128},{64,192},{128,0},{192,64},{1,129},{65,193},{129,1},{193,65... | collective-permute-start | bytes 196616 | tf_op jit(solution)/shard_map/ppermute | solution.py:26
  98.0 1.9 %collective-permute-done.37.refs_3_ = bf16[4,16,512]{2,1,0:T(8,128)(2,1)S(1)} collective-permute-done((bf16[4,16,512]{2,1,0:T(8,128)(2,1)S(1)}, bf16[4,16,512]{2,1,0:T(8,128)(2,1)S(1)}, u32[]{:S(2)}, u32[]{:S(2)}) %collective-permute-start.37) | collective-permute-done | bytes 65568 | tf_op jit(solution)/shard_map/ppermute | solution.py:26
  100.0 3.3 %collective-permute-done.36.refs_2_ = bf16[4,16,512]{2,1,0:T(8,128)(2,1)S(1)} collective-permute-done((bf16[4,16,512]{2,1,0:T(8,128)(2,1)S(1)}, bf16[4,16,512]{2,1,0:T(8,128)(2,1)S(1)}, u32[]{:S(2)}, u32[]{:S(2)}) %collective-permute-start.36) | collective-permute-done | bytes 65568 | tf_op jit(solution)/shard_map/ppermute | solution.py:26
  103.3 1.5 collective-permute-start.40
  104.8 2.4 %collective-permute-start.39 = (bf16[4,4,16,512]{3,2,1,0:T(8,128)(2,1)S(1)}, bf16[4,4,16,512]{3,2,1,0:T(8,128)(2,1)S(1)}, u32[]{:S(2)}, u32[]{:S(2)}) collective-permute-start(bf16[4,4,16,512]{3,2,1,0:T(8,128)(2,1)S(1)} %joined.11.refs_0_), channel_id=1, source_target_pairs={{0,32},{16,48},{32,0},{48,16},{1,33},{17,49},{33,1},{49,17},{2,34}... | collective-permute-start | bytes 786440 | tf_op jit(solution)/shard_map/ppermute | solution.py:21
  110.6 7.3 %collective-permute-done.25.refs_1_ = bf16[2,2,16,512]{3,2,1,0:T(8,128)(2,1)S(1)} collective-permute-done((bf16[2,2,16,512]{3,2,1,0:T(8,128)(2,1)S(1)}, bf16[2,2,16,512]{3,2,1,0:T(8,128)(2,1)S(1)}, u32[]{:S(2)}, u32[]{:S(2)}) %collective-permute-start.25) | collective-permute-done | bytes 65568 | tf_op jit(solution)/shard_map/ppermute | solution.py:31
  118.9 1.8 %collective-permute-start.27 = (bf16[2,2,2,16,512]{4,3,2,1,0:T(8,128)(2,1)S(1)}, bf16[2,2,2,16,512]{4,3,2,1,0:T(8,128)(2,1)S(1)}, u32[]{:S(2)}, u32[]{:S(2)}) collective-permute-start(bf16[2,2,2,16,512]{4,3,2,1,0:T(8,128)(2,1)S(1)} %joined.10.refs_0_), channel_id=1, source_target_pairs={{0,4},{2,6},{4,0},{6,2},{1,5},{3,7},{5,1},{7,3},{8,12},{10,14},{12... | collective-permute-start | bytes 393224 | tf_op jit(solution)/shard_map/ppermute | solution.py:21
  120.6 2.5 %collective-permute-start.26 = (bf16[2,2,2,16,512]{4,3,2,1,0:T(8,128)(2,1)S(1)}, bf16[2,2,2,16,512]{4,3,2,1,0:T(8,128)(2,1)S(1)}, u32[]{:S(2)}, u32[]{:S(2)}) collective-permute-start(bf16[2,2,2,16,512]{4,3,2,1,0:T(8,128)(2,1)S(1)} %joined.10.refs_0_), channel_id=1, source_target_pairs={{0,2},{2,4},{4,6},{6,0},{1,3},{3,5},{5,7},{7,1},{8,10},{10,12},{12... | collective-permute-start | bytes 393224 | tf_op jit(solution)/shard_map/ppermute | solution.py:21
  124.6 1.7 %collective-permute-done.27.refs_2_ = bf16[2,2,2,16,512]{4,3,2,1,0:T(8,128)(2,1)S(1)} collective-permute-done((bf16[2,2,2,16,512]{4,3,2,1,0:T(8,128)(2,1)S(1)}, bf16[2,2,2,16,512]{4,3,2,1,0:T(8,128)(2,1)S(1)}, u32[]{:S(2)}, u32[]{:S(2)}) %collective-permute-start.27) | collective-permute-done | bytes 131104 | tf_op jit(solution)/shard_map/ppermute | solution.py:21
  126.3 2.1 %collective-permute-done.26.refs_1_ = bf16[2,2,2,16,512]{4,3,2,1,0:T(8,128)(2,1)S(1)} collective-permute-done((bf16[2,2,2,16,512]{4,3,2,1,0:T(8,128)(2,1)S(1)}, bf16[2,2,2,16,512]{4,3,2,1,0:T(8,128)(2,1)S(1)}, u32[]{:S(2)}, u32[]{:S(2)}) %collective-permute-start.26) | collective-permute-done | bytes 131104 | tf_op jit(solution)/shard_map/ppermute | solution.py:21
  128.4 1.9 %cols_product.3 = (f32[4,4,16,512]{3,2,1,0:T(8,128)S(1)}, bf16[4,4,16,512]{3,2,1,0:T(8,128)(2,1)S(1)}, bf16[4,4,16,512]{3,2,1,0:T(8,128)(2,1)S(1)}, bf16[4,4,16,512]{3,2,1,0:T(8,128)(2,1)S(1)}) custom-call(bf16[2,2,2,16,512]{4,3,2,1,0:T(8,128)(2,1)S(1)} %joined.10.refs_0_, bf16[2,2,2,16,512]{4,3,2,1,0:T(8,128)(2,1)S(1)} %collective-permute-done.26.refs_1_, ...), custom_call_target="tpu_custom_call" | custom-call | tf_op jit(solution)/shard_map/cols_product/pallas_call | solution.py:174
  130.4 1.6 %collective-permute-start.29 = (bf16[4,4,16,512]{3,2,1,0:T(8,128)(2,1)S(1)}, bf16[4,4,16,512]{3,2,1,0:T(8,128)(2,1)S(1)}, u32[]{:S(2)}, u32[]{:S(2)}) collective-permute-start(bf16[4,4,16,512]{3,2,1,0:T(8,128)(2,1)S(1)} %get-tuple-element.58), channel_id=1, source_target_pairs={{0,16},{16,32},{32,48},{48,0},{1,17},{17,33},{33,49},{49,1},{2,18}... | collective-permute-start | bytes 786440 | tf_op jit(solution)/shard_map/ppermute | solution.py:21
  132.0 1.8 %collective-permute-start.30 = (bf16[4,4,16,512]{3,2,1,0:T(8,128)(2,1)S(1)}, bf16[4,4,16,512]{3,2,1,0:T(8,128)(2,1)S(1)}, u32[]{:S(2)}, u32[]{:S(2)}) collective-permute-start(bf16[4,4,16,512]{3,2,1,0:T(8,128)(2,1)S(1)} %get-tuple-element.59), channel_id=1, source_target_pairs={{0,48},{16,0},{32,16},{48,32},{1,49},{17,1},{33,17},{49,33},{2,50}... | collective-permute-start | bytes 786440 | tf_op jit(solution)/shard_map/ppermute | solution.py:21
  133.8 1.7 %collective-permute-start.31 = (bf16[4,4,16,512]{3,2,1,0:T(8,128)(2,1)S(1)}, bf16[4,4,16,512]{3,2,1,0:T(8,128)(2,1)S(1)}, u32[]{:S(2)}, u32[]{:S(2)}) collective-permute-start(bf16[4,4,16,512]{3,2,1,0:T(8,128)(2,1)S(1)} %get-tuple-element.60), channel_id=1, source_target_pairs={{0,32},{16,48},{32,0},{48,16},{1,33},{17,49},{33,1},{49,17},{2,34}... | collective-permute-start | bytes 786440 | tf_op jit(solution)/shard_map/ppermute | solution.py:21
  135.5 1.6 %collective-permute-start.42 = (bf16[2,2,2,16,512]{4,3,2,1,0:T(8,128)(2,1)S(1)}, bf16[2,2,2,16,512]{4,3,2,1,0:T(8,128)(2,1)S(1)}, u32[]{:S(2)}, u32[]{:S(2)}) collective-permute-start(bf16[2,2,2,16,512]{4,3,2,1,0:T(8,128)(2,1)S(1)} %get-tuple-element.68), channel_id=1, source_target_pairs={{0,6},{2,0},{4,2},{6,4},{1,7},{3,1},{5,3},{7,5},{8,14},{10,8},{12,... | collective-permute-start | bytes 393224 | tf_op jit(solution)/shard_map/ppermute | solution.py:21
  137.7 3.4 %collective-permute-done.42.refs_2_ = bf16[2,2,2,16,512]{4,3,2,1,0:T(8,128)(2,1)S(1)} collective-permute-done((bf16[2,2,2,16,512]{4,3,2,1,0:T(8,128)(2,1)S(1)}, bf16[2,2,2,16,512]{4,3,2,1,0:T(8,128)(2,1)S(1)}, u32[]{:S(2)}, u32[]{:S(2)}) %collective-permute-start.42) | collective-permute-done | bytes 131104 | tf_op jit(solution)/shard_map/ppermute | solution.py:21
  141.1 2.5 %collective-permute-done.43.refs_3_ = bf16[2,2,2,16,512]{4,3,2,1,0:T(8,128)(2,1)S(1)} collective-permute-done((bf16[2,2,2,16,512]{4,3,2,1,0:T(8,128)(2,1)S(1)}, bf16[2,2,2,16,512]{4,3,2,1,0:T(8,128)(2,1)S(1)}, u32[]{:S(2)}, u32[]{:S(2)}) %collective-permute-start.43) | collective-permute-done | bytes 131104 | tf_op jit(solution)/shard_map/ppermute | solution.py:21
  144.6 2.6 %collective-permute-start.33 = (bf16[4,16,512]{2,1,0:T(8,128)(2,1)S(1)}, bf16[4,16,512]{2,1,0:T(8,128)(2,1)S(1)}, u32[]{:S(2)}, u32[]{:S(2)}) collective-permute-start(bf16[4,16,512]{2,1,0:T(8,128)(2,1)S(1)} %get-tuple-element.63), channel_id=1, source_target_pairs={{0,128},{64,192},{128,0},{192,64},{1,129},{65,193},{129,1},{193,65... | collective-permute-start | bytes 196616 | tf_op jit(solution)/shard_map/ppermute | solution.py:26
  147.2 1.8 %collective-permute-start.34 = (bf16[4,16,512]{2,1,0:T(8,128)(2,1)S(1)}, bf16[4,16,512]{2,1,0:T(8,128)(2,1)S(1)}, u32[]{:S(2)}, u32[]{:S(2)}) collective-permute-start(bf16[4,16,512]{2,1,0:T(8,128)(2,1)S(1)} %get-tuple-element.64), channel_id=1, source_target_pairs={{0,192},{64,128},{128,64},{192,0},{1,193},{65,129},{129,65},{193,1... | collective-permute-start | bytes 196616 | tf_op jit(solution)/shard_map/ppermute | solution.py:26
  150.7 4.4 %collective-permute-done.33.refs_6_ = bf16[4,16,512]{2,1,0:T(8,128)(2,1)S(1)} collective-permute-done((bf16[4,16,512]{2,1,0:T(8,128)(2,1)S(1)}, bf16[4,16,512]{2,1,0:T(8,128)(2,1)S(1)}, u32[]{:S(2)}, u32[]{:S(2)}) %collective-permute-start.33) | collective-permute-done | bytes 65568 | tf_op jit(solution)/shard_map/ppermute | solution.py:26
  155.1 2.2 %collective-permute-done.45.refs_8_ = bf16[4,16,512]{2,1,0:T(8,128)(2,1)S(1)} collective-permute-done((bf16[4,16,512]{2,1,0:T(8,128)(2,1)S(1)}, bf16[4,16,512]{2,1,0:T(8,128)(2,1)S(1)}, u32[]{:S(2)}, u32[]{:S(2)}) %collective-permute-start.45) | collective-permute-done | bytes 65568 | tf_op jit(solution)/shard_map/ppermute | solution.py:31
  (86 shorter events, 21.8 us)
Async XLA Ops:
  4.0 32.6 %collective-permute-start.18 = (bf16[2048,512]{1,0:T(8,128)(2,1)S(1)}, bf16[2048,512]{1,0:T(8,128)(2,1)S(1)}, u32[]{:S(2)}, u32[]{:S(2)}) collective-permute-start(bf16[2048,512]{1,0:T(8,128)(2,1)S(1)} %mask_tile.3.refs_4_), channel_id=1, source_target_pairs={{0,8},{8,0},{1,9},{9,1},{2,10},{10,2},{3,11},{11,3},{4,12},{12,4},... | collective-permute-start | bytes 6291464 | tf_op jit(solution)/shard_map/ppermute | solution.py:31
  5.6 44.7 %collective-permute-start.5 = (bf16[512,2048]{1,0:T(8,128)(2,1)S(1)}, bf16[512,2048]{1,0:T(8,128)(2,1)S(1)}, u32[]{:S(2)}, u32[]{:S(2)}) collective-permute-start(bf16[512,2048]{1,0:T(8,128)(2,1)S(1)} %mask_tile.2.refs_4_), channel_id=1, source_target_pairs={{0,8},{8,0},{1,9},{9,1},{2,10},{10,2},{3,11},{11,3},{4,12},{12,4},... | collective-permute-start | bytes 6291464 | tf_op jit(solution)/shard_map/ppermute | solution.py:31
  5.9 7.7 %collective-permute-start.14 = (bf16[4,16,512]{2,1,0:T(8,128)(2,1)S(1)}, bf16[4,16,512]{2,1,0:T(8,128)(2,1)S(1)}, u32[]{:S(2)}, u32[]{:S(2)}) collective-permute-start(bf16[4,16,512]{2,1,0:T(8,128)(2,1)S(1)} %get-tuple-element.47.refs_0_), channel_id=1, source_target_pairs={{0,192},{64,128},{128,64},{192,0},{1,193},{65,129},{129,65},{193,1... | collective-permute-start | bytes 196616 | tf_op jit(solution)/shard_map/ppermute | solution.py:26
  10.7 5.6 %collective-permute-start.13 = (bf16[4,16,512]{2,1,0:T(8,128)(2,1)S(1)}, bf16[4,16,512]{2,1,0:T(8,128)(2,1)S(1)}, u32[]{:S(2)}, u32[]{:S(2)}) collective-permute-start(bf16[4,16,512]{2,1,0:T(8,128)(2,1)S(1)} %get-tuple-element.47.refs_0_), channel_id=1, source_target_pairs={{0,128},{64,192},{128,0},{192,64},{1,129},{65,193},{129,1},{193,65... | collective-permute-start | bytes 196616 | tf_op jit(solution)/shard_map/ppermute | solution.py:26
  10.7 5.7 %collective-permute-start.12 = (bf16[4,16,512]{2,1,0:T(8,128)(2,1)S(1)}, bf16[4,16,512]{2,1,0:T(8,128)(2,1)S(1)}, u32[]{:S(2)}, u32[]{:S(2)}) collective-permute-start(bf16[4,16,512]{2,1,0:T(8,128)(2,1)S(1)} %get-tuple-element.47.refs_0_), channel_id=1, source_target_pairs={{0,64},{64,0},{128,192},{192,128},{1,65},{65,1},{129,193},{193,129... | collective-permute-start | bytes 196616 | tf_op jit(solution)/shard_map/ppermute | solution.py:26
  16.4 13.9 %collective-permute-start.17 = (bf16[4,4,16,512]{3,2,1,0:T(8,128)(2,1)S(1)}, bf16[4,4,16,512]{3,2,1,0:T(8,128)(2,1)S(1)}, u32[]{:S(2)}, u32[]{:S(2)}) collective-permute-start(bf16[4,4,16,512]{3,2,1,0:T(8,128)(2,1)S(1)} %joined.8.refs_0_), channel_id=1, source_target_pairs={{0,48},{16,0},{32,16},{48,32},{1,49},{17,1},{33,17},{49,33},{2,50}... | collective-permute-start | bytes 786440 | tf_op jit(solution)/shard_map/ppermute | solution.py:21
  19.2 1.2 collective-permute-start
  19.2 17.4 %collective-permute-start.16 = (bf16[4,4,16,512]{3,2,1,0:T(8,128)(2,1)S(1)}, bf16[4,4,16,512]{3,2,1,0:T(8,128)(2,1)S(1)}, u32[]{:S(2)}, u32[]{:S(2)}) collective-permute-start(bf16[4,4,16,512]{3,2,1,0:T(8,128)(2,1)S(1)} %joined.8.refs_0_), channel_id=1, source_target_pairs={{0,32},{16,48},{32,0},{48,16},{1,33},{17,49},{33,1},{49,17},{2,34}... | collective-permute-start | bytes 786440 | tf_op jit(solution)/shard_map/ppermute | solution.py:21
  20.4 16.2 %collective-permute-start.15 = (bf16[4,4,16,512]{3,2,1,0:T(8,128)(2,1)S(1)}, bf16[4,4,16,512]{3,2,1,0:T(8,128)(2,1)S(1)}, u32[]{:S(2)}, u32[]{:S(2)}) collective-permute-start(bf16[4,4,16,512]{3,2,1,0:T(8,128)(2,1)S(1)} %joined.8.refs_0_), channel_id=1, source_target_pairs={{0,16},{16,32},{32,48},{48,0},{1,17},{17,33},{33,49},{49,1},{2,18}... | collective-permute-start | bytes 786440 | tf_op jit(solution)/shard_map/ppermute | solution.py:21
  30.3 9.3 %collective-permute-start.1 = (bf16[2,2,16,512]{3,2,1,0:T(8,128)(2,1)S(1)}, bf16[2,2,16,512]{3,2,1,0:T(8,128)(2,1)S(1)}, u32[]{:S(2)}, u32[]{:S(2)}) collective-permute-start(bf16[2,2,16,512]{3,2,1,0:T(8,128)(2,1)S(1)} %joined.6.refs_0_), channel_id=1, source_target_pairs={{0,1},{1,0},{2,3},{3,2},{4,5},{5,4},{6,7},{7,6},{8,9},{9,8},{10,11... | collective-permute-start | bytes 196616 | tf_op jit(solution)/shard_map/ppermute | solution.py:31
  37.9 21.7 %collective-permute-start.19 = (f32[2,2,2,16,512]{4,3,2,1,0:T(8,128)S(1)}, f32[2,2,2,16,512]{4,3,2,1,0:T(8,128)S(1)}, u32[]{:S(2)}, u32[]{:S(2)}) collective-permute-start(f32[2,2,2,16,512]{4,3,2,1,0:T(8,128)S(1)} %get-tuple-element.49), channel_id=1, source_target_pairs={{0,2},{2,4},{4,6},{6,0},{1,3},{3,5},{5,7},{7,1},{8,10},{10,12},{12... | collective-permute-start | bytes 786440 | tf_op jit(solution)/shard_map/ppermute | solution.py:21
  39.6 5.8 %collective-permute-start.4 = (bf16[2,2,2,16,512]{4,3,2,1,0:T(8,128)(2,1)S(1)}, bf16[2,2,2,16,512]{4,3,2,1,0:T(8,128)(2,1)S(1)}, u32[]{:S(2)}, u32[]{:S(2)}) collective-permute-start(bf16[2,2,2,16,512]{4,3,2,1,0:T(8,128)(2,1)S(1)} %joined.7.refs_0_), channel_id=1, source_target_pairs={{0,6},{2,0},{4,2},{6,4},{1,7},{3,1},{5,3},{7,5},{8,14},{10,8},{12,... | collective-permute-start | bytes 393224 | tf_op jit(solution)/shard_map/ppermute | solution.py:21
  40.1 6.6 %collective-permute-start.3 = (bf16[2,2,2,16,512]{4,3,2,1,0:T(8,128)(2,1)S(1)}, bf16[2,2,2,16,512]{4,3,2,1,0:T(8,128)(2,1)S(1)}, u32[]{:S(2)}, u32[]{:S(2)}) collective-permute-start(bf16[2,2,2,16,512]{4,3,2,1,0:T(8,128)(2,1)S(1)} %joined.7.refs_0_), channel_id=1, source_target_pairs={{0,4},{2,6},{4,0},{6,2},{1,5},{3,7},{5,1},{7,3},{8,12},{10,14},{12... | collective-permute-start | bytes 393224 | tf_op jit(solution)/shard_map/ppermute | solution.py:21
  42.4 7.9 %collective-permute-start.2 = (bf16[2,2,2,16,512]{4,3,2,1,0:T(8,128)(2,1)S(1)}, bf16[2,2,2,16,512]{4,3,2,1,0:T(8,128)(2,1)S(1)}, u32[]{:S(2)}, u32[]{:S(2)}) collective-permute-start(bf16[2,2,2,16,512]{4,3,2,1,0:T(8,128)(2,1)S(1)} %joined.7.refs_0_), channel_id=1, source_target_pairs={{0,2},{2,4},{4,6},{6,0},{1,3},{3,5},{5,7},{7,1},{8,10},{10,12},{12... | collective-permute-start | bytes 393224 | tf_op jit(solution)/shard_map/ppermute | solution.py:21
  52.2 40.6 %copy-start.2 = (bf16[16,4,1,512]{3,1,2,0:T(4,128)(2,1)S(1)}, bf16[16,4,1,512]{3,1,2,0:T(4,128)(2,1)}, u32[]{:S(2)}) copy-start(bf16[16,4,1,512]{3,1,2,0:T(4,128)(2,1)} %param.11) | copy-start | bytes 196612
  52.2 40.6 %copy-start.4 = (f32[512]{0:T(512)S(1)}, f32[512]{0:T(512)}, u32[]{:S(2)}) copy-start(f32[512]{0:T(512)} %param.19) | copy-start | bytes 6148
  52.2 24.3 %collective-permute-start.6 = (f32[4,4,16,512]{3,2,1,0:T(8,128)S(1)}, f32[4,4,16,512]{3,2,1,0:T(8,128)S(1)}, u32[]{:S(2)}, u32[]{:S(2)}) collective-permute-start(f32[4,4,16,512]{3,2,1,0:T(8,128)S(1)} %get-tuple-element.40), channel_id=1, source_target_pairs={{0,16},{16,32},{32,48},{48,0},{1,17},{17,33},{33,49},{49,1},{2,18}... | collective-permute-start | bytes 1572872 | tf_op jit(solution)/shard_map/ppermute | solution.py:21
  52.3 24.6 %collective-permute-start.7 = (f32[4,4,16,512]{3,2,1,0:T(8,128)S(1)}, f32[4,4,16,512]{3,2,1,0:T(8,128)S(1)}, u32[]{:S(2)}, u32[]{:S(2)}) collective-permute-start(f32[4,4,16,512]{3,2,1,0:T(8,128)S(1)} %get-tuple-element.41), channel_id=1, source_target_pairs={{0,48},{16,0},{32,16},{48,32},{1,49},{17,1},{33,17},{49,33},{2,50}... | collective-permute-start | bytes 1572872 | tf_op jit(solution)/shard_map/ppermute | solution.py:21
  56.5 22.2 %collective-permute-start.8 = (f32[4,4,16,512]{3,2,1,0:T(8,128)S(1)}, f32[4,4,16,512]{3,2,1,0:T(8,128)S(1)}, u32[]{:S(2)}, u32[]{:S(2)}) collective-permute-start(f32[4,4,16,512]{3,2,1,0:T(8,128)S(1)} %get-tuple-element.42), channel_id=1, source_target_pairs={{0,32},{16,48},{32,0},{48,16},{1,33},{17,49},{33,1},{49,17},{2,34}... | collective-permute-start | bytes 1572872 | tf_op jit(solution)/shard_map/ppermute | solution.py:21
  57.9 8.8 %collective-permute-start.20 = (f32[2,2,2,16,512]{4,3,2,1,0:T(8,128)S(1)}, f32[2,2,2,16,512]{4,3,2,1,0:T(8,128)S(1)}, u32[]{:S(2)}, u32[]{:S(2)}) collective-permute-start(f32[2,2,2,16,512]{4,3,2,1,0:T(8,128)S(1)} %get-tuple-element.50), channel_id=1, source_target_pairs={{0,6},{2,0},{4,2},{6,4},{1,7},{3,1},{5,3},{7,5},{8,14},{10,8},{12,... | collective-permute-start | bytes 786440 | tf_op jit(solution)/shard_map/ppermute | solution.py:21
  59.6 9.9 %collective-permute-start.21 = (f32[2,2,2,16,512]{4,3,2,1,0:T(8,128)S(1)}, f32[2,2,2,16,512]{4,3,2,1,0:T(8,128)S(1)}, u32[]{:S(2)}, u32[]{:S(2)}) collective-permute-start(f32[2,2,2,16,512]{4,3,2,1,0:T(8,128)S(1)} %get-tuple-element.51), channel_id=1, source_target_pairs={{0,4},{2,6},{4,0},{6,2},{1,5},{3,7},{5,1},{7,3},{8,12},{10,14},{12... | collective-permute-start | bytes 786440 | tf_op jit(solution)/shard_map/ppermute | solution.py:21
  69.5 1.4 collective-permute-start.22
  71.0 12.3 %collective-permute-start.23 = (f32[4,16,512]{2,1,0:T(8,128)S(1)}, f32[4,16,512]{2,1,0:T(8,128)S(1)}, u32[]{:S(2)}, u32[]{:S(2)}) collective-permute-start(f32[4,16,512]{2,1,0:T(8,128)S(1)} %woven.2), channel_id=1, source_target_pairs={{0,1},{1,0},{2,3},{3,2},{4,5},{5,4},{6,7},{7,6},{8,9},{9,8},{10,11... | collective-permute-start | bytes 393224 | tf_op jit(solution)/shard_map/ppermute | solution.py:31
  78.8 9.6 %collective-permute-start.9 = (f32[4,16,512]{2,1,0:T(8,128)S(1)}, f32[4,16,512]{2,1,0:T(8,128)S(1)}, u32[]{:S(2)}, u32[]{:S(2)}) collective-permute-start(f32[4,16,512]{2,1,0:T(8,128)S(1)} %get-tuple-element.44), channel_id=1, source_target_pairs={{0,64},{64,0},{128,192},{192,128},{1,65},{65,1},{129,193},{193,129... | collective-permute-start | bytes 393224 | tf_op jit(solution)/shard_map/ppermute | solution.py:26
  79.5 13.3 %collective-permute-start.10 = (f32[4,16,512]{2,1,0:T(8,128)S(1)}, f32[4,16,512]{2,1,0:T(8,128)S(1)}, u32[]{:S(2)}, u32[]{:S(2)}) collective-permute-start(f32[4,16,512]{2,1,0:T(8,128)S(1)} %get-tuple-element.45), channel_id=1, source_target_pairs={{0,128},{64,192},{128,0},{192,64},{1,129},{65,193},{129,1},{193,65... | collective-permute-start | bytes 393224 | tf_op jit(solution)/shard_map/ppermute | solution.py:26
  81.3 11.5 %collective-permute-start.11 = (f32[4,16,512]{2,1,0:T(8,128)S(1)}, f32[4,16,512]{2,1,0:T(8,128)S(1)}, u32[]{:S(2)}, u32[]{:S(2)}) collective-permute-start(f32[4,16,512]{2,1,0:T(8,128)S(1)} %get-tuple-element.46), channel_id=1, source_target_pairs={{0,192},{64,128},{128,64},{192,0},{1,193},{65,129},{129,65},{193,1... | collective-permute-start | bytes 393224 | tf_op jit(solution)/shard_map/ppermute | solution.py:26
  93.5 6.4 %collective-permute-start.37 = (bf16[4,16,512]{2,1,0:T(8,128)(2,1)S(1)}, bf16[4,16,512]{2,1,0:T(8,128)(2,1)S(1)}, u32[]{:S(2)}, u32[]{:S(2)}) collective-permute-start(bf16[4,16,512]{2,1,0:T(8,128)(2,1)S(1)} %get-tuple-element.65.refs_0_), channel_id=1, source_target_pairs={{0,192},{64,128},{128,64},{192,0},{1,193},{65,129},{129,65},{193,1... | collective-permute-start | bytes 196616 | tf_op jit(solution)/shard_map/ppermute | solution.py:26
  95.1 8.1 %collective-permute-start.36 = (bf16[4,16,512]{2,1,0:T(8,128)(2,1)S(1)}, bf16[4,16,512]{2,1,0:T(8,128)(2,1)S(1)}, u32[]{:S(2)}, u32[]{:S(2)}) collective-permute-start(bf16[4,16,512]{2,1,0:T(8,128)(2,1)S(1)} %get-tuple-element.65.refs_0_), channel_id=1, source_target_pairs={{0,128},{64,192},{128,0},{192,64},{1,129},{65,193},{129,1},{193,65... | collective-permute-start | bytes 196616 | tf_op jit(solution)/shard_map/ppermute | solution.py:26
  98.0 5.2 %collective-permute-start.35 = (bf16[4,16,512]{2,1,0:T(8,128)(2,1)S(1)}, bf16[4,16,512]{2,1,0:T(8,128)(2,1)S(1)}, u32[]{:S(2)}, u32[]{:S(2)}) collective-permute-start(bf16[4,16,512]{2,1,0:T(8,128)(2,1)S(1)} %get-tuple-element.65.refs_0_), channel_id=1, source_target_pairs={{0,64},{64,0},{128,192},{192,128},{1,65},{65,1},{129,193},{193,129... | collective-permute-start | bytes 196616 | tf_op jit(solution)/shard_map/ppermute | solution.py:26
  103.3 17.4 %collective-permute-start.40 = (bf16[4,4,16,512]{3,2,1,0:T(8,128)(2,1)S(1)}, bf16[4,4,16,512]{3,2,1,0:T(8,128)(2,1)S(1)}, u32[]{:S(2)}, u32[]{:S(2)}) collective-permute-start(bf16[4,4,16,512]{3,2,1,0:T(8,128)(2,1)S(1)} %joined.11.refs_0_), channel_id=1, source_target_pairs={{0,48},{16,0},{32,16},{48,32},{1,49},{17,1},{33,17},{49,33},{2,50}... | collective-permute-start | bytes 786440 | tf_op jit(solution)/shard_map/ppermute | solution.py:21
  104.8 18.4 %collective-permute-start.39 = (bf16[4,4,16,512]{3,2,1,0:T(8,128)(2,1)S(1)}, bf16[4,4,16,512]{3,2,1,0:T(8,128)(2,1)S(1)}, u32[]{:S(2)}, u32[]{:S(2)}) collective-permute-start(bf16[4,4,16,512]{3,2,1,0:T(8,128)(2,1)S(1)} %joined.11.refs_0_), channel_id=1, source_target_pairs={{0,32},{16,48},{32,0},{48,16},{1,33},{17,49},{33,1},{49,17},{2,34}... | collective-permute-start | bytes 786440 | tf_op jit(solution)/shard_map/ppermute | solution.py:21
  107.2 16.0 %collective-permute-start.38 = (bf16[4,4,16,512]{3,2,1,0:T(8,128)(2,1)S(1)}, bf16[4,4,16,512]{3,2,1,0:T(8,128)(2,1)S(1)}, u32[]{:S(2)}, u32[]{:S(2)}) collective-permute-start(bf16[4,4,16,512]{3,2,1,0:T(8,128)(2,1)S(1)} %joined.11.refs_0_), channel_id=1, source_target_pairs={{0,16},{16,32},{32,48},{48,0},{1,17},{17,33},{33,49},{49,1},{2,18}... | collective-permute-start | bytes 786440 | tf_op jit(solution)/shard_map/ppermute | solution.py:21
  108.5 1.2 collective-permute-start.24
  109.7 8.2 %collective-permute-start.25 = (bf16[2,2,16,512]{3,2,1,0:T(8,128)(2,1)S(1)}, bf16[2,2,16,512]{3,2,1,0:T(8,128)(2,1)S(1)}, u32[]{:S(2)}, u32[]{:S(2)}) collective-permute-start(bf16[2,2,16,512]{3,2,1,0:T(8,128)(2,1)S(1)} %joined.9.refs_0_), channel_id=1, source_target_pairs={{0,1},{1,0},{2,3},{3,2},{4,5},{5,4},{6,7},{7,6},{8,9},{9,8},{10,11... | collective-permute-start | bytes 196616 | tf_op jit(solution)/shard_map/ppermute | solution.py:31
  117.9 6.7 %collective-permute-start.28 = (bf16[2,2,2,16,512]{4,3,2,1,0:T(8,128)(2,1)S(1)}, bf16[2,2,2,16,512]{4,3,2,1,0:T(8,128)(2,1)S(1)}, u32[]{:S(2)}, u32[]{:S(2)}) collective-permute-start(bf16[2,2,2,16,512]{4,3,2,1,0:T(8,128)(2,1)S(1)} %joined.10.refs_0_), channel_id=1, source_target_pairs={{0,6},{2,0},{4,2},{6,4},{1,7},{3,1},{5,3},{7,5},{8,14},{10,8},{12,... | collective-permute-start | bytes 393224 | tf_op jit(solution)/shard_map/ppermute | solution.py:21
  118.9 7.4 %collective-permute-start.27 = (bf16[2,2,2,16,512]{4,3,2,1,0:T(8,128)(2,1)S(1)}, bf16[2,2,2,16,512]{4,3,2,1,0:T(8,128)(2,1)S(1)}, u32[]{:S(2)}, u32[]{:S(2)}) collective-permute-start(bf16[2,2,2,16,512]{4,3,2,1,0:T(8,128)(2,1)S(1)} %joined.10.refs_0_), channel_id=1, source_target_pairs={{0,4},{2,6},{4,0},{6,2},{1,5},{3,7},{5,1},{7,3},{8,12},{10,14},{12... | collective-permute-start | bytes 393224 | tf_op jit(solution)/shard_map/ppermute | solution.py:21
  120.6 7.8 %collective-permute-start.26 = (bf16[2,2,2,16,512]{4,3,2,1,0:T(8,128)(2,1)S(1)}, bf16[2,2,2,16,512]{4,3,2,1,0:T(8,128)(2,1)S(1)}, u32[]{:S(2)}, u32[]{:S(2)}) collective-permute-start(bf16[2,2,2,16,512]{4,3,2,1,0:T(8,128)(2,1)S(1)} %joined.10.refs_0_), channel_id=1, source_target_pairs={{0,2},{2,4},{4,6},{6,0},{1,3},{3,5},{5,7},{7,1},{8,10},{10,12},{12... | collective-permute-start | bytes 393224 | tf_op jit(solution)/shard_map/ppermute | solution.py:21
  124.5 12.6 %collective-permute-start.41 = (bf16[2,2,2,16,512]{4,3,2,1,0:T(8,128)(2,1)S(1)}, bf16[2,2,2,16,512]{4,3,2,1,0:T(8,128)(2,1)S(1)}, u32[]{:S(2)}, u32[]{:S(2)}) collective-permute-start(bf16[2,2,2,16,512]{4,3,2,1,0:T(8,128)(2,1)S(1)} %get-tuple-element.67), channel_id=1, source_target_pairs={{0,2},{2,4},{4,6},{6,0},{1,3},{3,5},{5,7},{7,1},{8,10},{10,12},{12... | collective-permute-start | bytes 393224 | tf_op jit(solution)/shard_map/ppermute | solution.py:21
  130.4 13.4 %collective-permute-start.29 = (bf16[4,4,16,512]{3,2,1,0:T(8,128)(2,1)S(1)}, bf16[4,4,16,512]{3,2,1,0:T(8,128)(2,1)S(1)}, u32[]{:S(2)}, u32[]{:S(2)}) collective-permute-start(bf16[4,4,16,512]{3,2,1,0:T(8,128)(2,1)S(1)} %get-tuple-element.58), channel_id=1, source_target_pairs={{0,16},{16,32},{32,48},{48,0},{1,17},{17,33},{33,49},{49,1},{2,18}... | collective-permute-start | bytes 786440 | tf_op jit(solution)/shard_map/ppermute | solution.py:21
  132.0 11.8 %collective-permute-start.30 = (bf16[4,4,16,512]{3,2,1,0:T(8,128)(2,1)S(1)}, bf16[4,4,16,512]{3,2,1,0:T(8,128)(2,1)S(1)}, u32[]{:S(2)}, u32[]{:S(2)}) collective-permute-start(bf16[4,4,16,512]{3,2,1,0:T(8,128)(2,1)S(1)} %get-tuple-element.59), channel_id=1, source_target_pairs={{0,48},{16,0},{32,16},{48,32},{1,49},{17,1},{33,17},{49,33},{2,50}... | collective-permute-start | bytes 786440 | tf_op jit(solution)/shard_map/ppermute | solution.py:21
  133.8 10.6 %collective-permute-start.31 = (bf16[4,4,16,512]{3,2,1,0:T(8,128)(2,1)S(1)}, bf16[4,4,16,512]{3,2,1,0:T(8,128)(2,1)S(1)}, u32[]{:S(2)}, u32[]{:S(2)}) collective-permute-start(bf16[4,4,16,512]{3,2,1,0:T(8,128)(2,1)S(1)} %get-tuple-element.60), channel_id=1, source_target_pairs={{0,32},{16,48},{32,0},{48,16},{1,33},{17,49},{33,1},{49,17},{2,34}... | collective-permute-start | bytes 786440 | tf_op jit(solution)/shard_map/ppermute | solution.py:21
  135.5 5.6 %collective-permute-start.42 = (bf16[2,2,2,16,512]{4,3,2,1,0:T(8,128)(2,1)S(1)}, bf16[2,2,2,16,512]{4,3,2,1,0:T(8,128)(2,1)S(1)}, u32[]{:S(2)}, u32[]{:S(2)}) collective-permute-start(bf16[2,2,2,16,512]{4,3,2,1,0:T(8,128)(2,1)S(1)} %get-tuple-element.68), channel_id=1, source_target_pairs={{0,6},{2,0},{4,2},{6,4},{1,7},{3,1},{5,3},{7,5},{8,14},{10,8},{12,... | collective-permute-start | bytes 393224 | tf_op jit(solution)/shard_map/ppermute | solution.py:21
  137.1 6.5 %collective-permute-start.43 = (bf16[2,2,2,16,512]{4,3,2,1,0:T(8,128)(2,1)S(1)}, bf16[2,2,2,16,512]{4,3,2,1,0:T(8,128)(2,1)S(1)}, u32[]{:S(2)}, u32[]{:S(2)}) collective-permute-start(bf16[2,2,2,16,512]{4,3,2,1,0:T(8,128)(2,1)S(1)} %get-tuple-element.69), channel_id=1, source_target_pairs={{0,4},{2,6},{4,0},{6,2},{1,5},{3,7},{5,1},{7,3},{8,12},{10,14},{12... | collective-permute-start | bytes 393224 | tf_op jit(solution)/shard_map/ppermute | solution.py:21
  143.7 5.3 %collective-permute-start.44 = (f32[2,2,16,512]{3,2,1,0:T(8,128)S(1)}, f32[2,2,16,512]{3,2,1,0:T(8,128)S(1)}, u32[]{:S(2)}, u32[]{:S(2)}) collective-permute-start(f32[2,2,16,512]{3,2,1,0:T(8,128)S(1)} %get-tuple-element.71), channel_id=1, source_target_pairs={{0,8},{8,0},{1,9},{9,1},{2,10},{10,2},{3,11},{11,3},{4,12},{12,4},... | collective-permute-start | bytes 393224 | tf_op jit(solution)/shard_map/ppermute | solution.py:31
  144.5 6.2 %collective-permute-start.32 = (bf16[4,16,512]{2,1,0:T(8,128)(2,1)S(1)}, bf16[4,16,512]{2,1,0:T(8,128)(2,1)S(1)}, u32[]{:S(2)}, u32[]{:S(2)}) collective-permute-start(bf16[4,16,512]{2,1,0:T(8,128)(2,1)S(1)} %get-tuple-element.62), channel_id=1, source_target_pairs={{0,64},{64,0},{128,192},{192,128},{1,65},{65,1},{129,193},{193,129... | collective-permute-start | bytes 196616 | tf_op jit(solution)/shard_map/ppermute | solution.py:26
  144.6 10.5 %collective-permute-start.33 = (bf16[4,16,512]{2,1,0:T(8,128)(2,1)S(1)}, bf16[4,16,512]{2,1,0:T(8,128)(2,1)S(1)}, u32[]{:S(2)}, u32[]{:S(2)}) collective-permute-start(bf16[4,16,512]{2,1,0:T(8,128)(2,1)S(1)} %get-tuple-element.63), channel_id=1, source_target_pairs={{0,128},{64,192},{128,0},{192,64},{1,129},{65,193},{129,1},{193,65... | collective-permute-start | bytes 196616 | tf_op jit(solution)/shard_map/ppermute | solution.py:26
  147.2 8.0 %collective-permute-start.34 = (bf16[4,16,512]{2,1,0:T(8,128)(2,1)S(1)}, bf16[4,16,512]{2,1,0:T(8,128)(2,1)S(1)}, u32[]{:S(2)}, u32[]{:S(2)}) collective-permute-start(bf16[4,16,512]{2,1,0:T(8,128)(2,1)S(1)} %get-tuple-element.64), channel_id=1, source_target_pairs={{0,192},{64,128},{128,64},{192,0},{1,193},{65,129},{129,65},{193,1... | collective-permute-start | bytes 196616 | tf_op jit(solution)/shard_map/ppermute | solution.py:26
  149.0 8.4 %collective-permute-start.45 = (bf16[4,16,512]{2,1,0:T(8,128)(2,1)S(1)}, bf16[4,16,512]{2,1,0:T(8,128)(2,1)S(1)}, u32[]{:S(2)}, u32[]{:S(2)}) collective-permute-start(bf16[4,16,512]{2,1,0:T(8,128)(2,1)S(1)} %woven.3), channel_id=1, source_target_pairs={{0,1},{1,0},{2,3},{3,2},{4,5},{5,4},{6,7},{7,6},{8,9},{9,8},{10,11... | collective-permute-start | bytes 196616 | tf_op jit(solution)/shard_map/ppermute | solution.py:31
  (8 other events, 129.2 us)
